TPU v7x, 32 devices: a whole 2x2x4 slice. The times are simulated.
32 devices in a mesh: query: 2 (over core), key: 2 (over x), heads: 8 (over z, y).
Axes of the slice: x: 2, y: 2, z: 4, core: 2. Of those that a mesh axis runs over, the one named last changes fastest.
Arguments:
- pair_feats: bfloat16 [1024, 64, 2048], P(('query', 'heads'), None, 'key'), may hold values from -6 to 6
- bucket_ids: int32 [1024, 2048], P(('query', 'heads'), 'key'), may hold values from 0 to 31
- ln_gain: float32 [64], replicated, may hold values from 0.5 to 1.5
- w_in: bfloat16 [64, 256], replicated, may hold values from -0.75 to 0.75
- b_in: float32 [256], replicated, may hold values from -3 to 3
- w_out: bfloat16 [256, 8], replicated, may hold values from -0.375 to 0.375
- bucket_table: bfloat16 [32, 8], replicated, may hold values from -4 to 4
- key_mask: int32 [2048], P('key'), may hold values 0 or 1
- q_heads: bfloat16 [8, 32, 1024], P('heads', None, 'query'), may hold values from -6 to 6
- k_heads: bfloat16 [8, 32, 2048], P('heads', None, 'key'), may hold values from -6 to 6
- v_heads: bfloat16 [8, 32, 2048], P('heads', None, 'key'), may hold values from -6 to 6
- out_heads: bfloat16 [8, 32, 1024], P('heads', None, 'query'), may hold values from -6 to 6
- dout_heads: bfloat16 [8, 32, 1024], P('heads', None, 'query'), may hold values from -96 to 96
- log_norm: float32 [8, 1024], P('heads', 'query'), may hold values from 8 to 10
Outputs:
- grad_pairs: bfloat16 [1024, 64, 2048], P(('query', 'heads'), None, 'key')
- grad_q: bfloat16 [8, 32, 1024], P('heads', None, 'query')
- grad_k: bfloat16 [8, 32, 2048], P('heads', None, 'key')
- grad_v: bfloat16 [8, 32, 2048], P('heads', None, 'key')
All inputs are finite; a program needn't handle non-finite values. No bound on the sum of `key_mask` on one device may be relied on, other than what follows from the above.
Results may differ from a plain program's by a relative error of at most 0.012.
The roundings to bfloat16 on the way count: a program that leaves them out, or rounds other values in their place, can miss the bound.
Values may be sent and summed in bfloat16 or wider, within the bound.
No kernel may reach another device: no remote copies, remote signals or barrier semaphores. Data moves between devices by JAX's collectives and lax.ppermute only.
A program may use at most 128 MiB of HBM per device.

v0:
```python
import math

import jax
import jax.numpy as jnp
from jax import lax
from jax.sharding import PartitionSpec as P


def gelu_parts(pre_act):
    cdf_val = 0.5 * (1.0 + jax.scipy.special.erf(pre_act * (1.0 / math.sqrt(2.0))))
    density = jnp.exp(-0.5 * pre_act * pre_act) * (1.0 / math.sqrt(2.0 * math.pi))
    return (pre_act * cdf_val, cdf_val + pre_act * density)


def normalize(pair_blk, ln_gain):
    values = pair_blk.astype(jnp.float32)
    centre = values - jnp.mean(values, axis=1, keepdims=True)
    inv_std = lax.rsqrt(jnp.mean(centre * centre, axis=1, keepdims=True) + 1e-05)
    unit_pairs = centre * inv_std
    normed = (unit_pairs * ln_gain[None, :, None]).astype(jnp.bfloat16)
    return (unit_pairs, inv_std, normed)


def by_groups(kernel_fn, arrays, group_rows):
    stacked = tuple(
        (
            member.reshape((member.shape[0] // group_rows, group_rows) + member.shape[1:])
            for member in arrays
        )
    )
    result = lax.map(lambda blocks: kernel_fn(*blocks), stacked)
    return jax.tree.map(
        lambda member: member.reshape((member.shape[0] * group_rows,) + member.shape[2:]), result
    )


def per_device(
    pair_feats,
    bucket_ids,
    ln_gain,
    w_in,
    b_in,
    w_out,
    bucket_table,
    key_mask,
    q_heads,
    k_heads,
    v_heads,
    out_heads,
    dout_heads,
    log_norm,
):
    pair_rows = pair_feats.shape[0]
    score_scale = 1.0 / math.sqrt(q_heads.shape[1])
    group_rows = math.gcd(pair_rows, 4)
    num_buckets = bucket_table.shape[0]
    deltas = jnp.sum(dout_heads.astype(jnp.float32) * out_heads.astype(jnp.float32), axis=1)
    delta_cols = jnp.transpose(deltas)[:, :, None]
    norm_cols = jnp.transpose(log_norm)[:, :, None]

    def forward_rows(pair_blk, bucket_blk):
        unit_pairs, inv_std, normed = normalize(pair_blk, ln_gain)
        pre_act = (
            jnp.einsum("rck,cf->rfk", normed, w_in, preferred_element_type=jnp.float32)
            + b_in[None, :, None]
        )
        gelu_val, gelu_slope = gelu_parts(pre_act)
        hidden = gelu_val.astype(jnp.bfloat16)
        bucket_iota = lax.broadcasted_iota(jnp.int32, (1, num_buckets, 1), 1)
        onehot = (bucket_blk[:, None, :] == bucket_iota).astype(jnp.bfloat16)
        lookup = jnp.einsum("rbk,bh->rhk", onehot, bucket_table, preferred_element_type=jnp.float32)
        mixed = jnp.einsum("rfk,fh->rhk", hidden, w_out, preferred_element_type=jnp.float32)
        return ((mixed + lookup).astype(jnp.bfloat16), unit_pairs, inv_std, normed)

    def backward_rows(unit_pairs, inv_std, normed, grad_blk):
        pre_act = (
            jnp.einsum("rck,cf->rfk", normed, w_in, preferred_element_type=jnp.float32)
            + b_in[None, :, None]
        )
        gelu_val, gelu_slope = gelu_parts(pre_act)
        dhidden = jnp.einsum("rhk,fh->rfk", grad_blk, w_out, preferred_element_type=jnp.float32)
        dpre = (dhidden * gelu_slope).astype(jnp.bfloat16)
        dunit = (
            jnp.einsum("rfk,cf->rck", dpre, w_in, preferred_element_type=jnp.float32)
            * ln_gain[None, :, None]
        )
        first_mean = jnp.mean(dunit, axis=1, keepdims=True)
        second_mean = jnp.mean(dunit * unit_pairs, axis=1, keepdims=True)
        return (inv_std * (dunit - first_mean - unit_pairs * second_mean)).astype(jnp.bfloat16)

    pair_blk = pair_feats
    bucket_blk = bucket_ids
    bias_vals, unit_pairs, inv_std, normed = by_groups(
        forward_rows, (pair_blk, bucket_blk), group_rows
    )
    bias_tile = lax.all_to_all(bias_vals, "heads", split_axis=1, concat_axis=0, tiled=True)
    scores = jnp.einsum(
        "hdi,hdj->ihj", q_heads, k_heads, preferred_element_type=jnp.float32
    ) * score_scale + bias_tile.astype(jnp.float32)
    attn_probs = jnp.where((key_mask == 1)[None, None, :], jnp.exp(scores - norm_cols), 0.0)
    probs_low = attn_probs.astype(jnp.bfloat16)
    dprobs = jnp.einsum("hdi,hdj->ihj", dout_heads, v_heads, preferred_element_type=jnp.float32)
    dscores = (attn_probs * (dprobs - delta_cols)).astype(jnp.bfloat16)
    dv_part = jnp.einsum("hdi,ihj->hdj", dout_heads, probs_low, preferred_element_type=jnp.float32)
    dk_part = jnp.einsum("hdi,ihj->hdj", q_heads, dscores, preferred_element_type=jnp.float32)
    dq_part = jnp.einsum("hdj,ihj->hdi", k_heads, dscores, preferred_element_type=jnp.float32)
    returned = lax.all_to_all(dscores, "heads", split_axis=0, concat_axis=1, tiled=True)
    grad_blk = by_groups(backward_rows, (unit_pairs, inv_std, normed, returned), group_rows)
    results = [(grad_blk, dk_part, dv_part, dq_part)]
    grad_pairs = jnp.concatenate([outcome[0] for outcome in results], axis=2)
    dk_cat = jnp.concatenate([outcome[1] for outcome in results], axis=2)
    dv_cat = jnp.concatenate([outcome[2] for outcome in results], axis=2)
    dq_total = results[0][3]
    dk_sum, dv_sum = lax.psum((dk_cat, dv_cat), "query")
    dq_sum = lax.psum(dq_total, "key")
    grad_q = (dq_sum * score_scale).astype(jnp.bfloat16)
    grad_k = (dk_sum * score_scale).astype(jnp.bfloat16)
    grad_v = dv_sum.astype(jnp.bfloat16)
    return (grad_pairs, grad_q, grad_k, grad_v)


def solution(mesh):
    return jax.shard_map(
        per_device,
        mesh=mesh,
        in_specs=(
            P(("query", "heads"), None, "key"),
            P(("query", "heads"), "key"),
            P(),
            P(),
            P(),
            P(),
            P(),
            P("key"),
            P("heads", None, "query"),
            P("heads", None, "key"),
            P("heads", None, "key"),
            P("heads", None, "query"),
            P("heads", None, "query"),
            P("heads", "query"),
        ),
        out_specs=(
            P(("query", "heads"), None, "key"),
            P("heads", None, "query"),
            P("heads", None, "key"),
            P("heads", None, "key"),
        ),
        check_vma=False,
    )
```

profile of v0, /device:TPU:0, one launch (start us, length us, event | category | flops | bytes accessed | tf_op | source)
XLA Modules:
  0.0 491.8 jit_solution(16679616385496339956)
XLA Ops:
  8.3 4.3 broadcast.105.clone
  12.6 170.9 %while.26 = (s32[]{:T(128)}, bf16[16,4,8,1024]{3,2,1,0:T(8,128)(2,1)S(1)}, f32[16,4,64,1024]{3,2,1,0:T(8,128)}, f32[16,4,1,1024]{3,1,2,0:T(4,128)}, bf16[16,4,64...) while((s32[]{:T(128)}, ...), condition=%wide.region_3.4_spmd, body=%wide.region_0.3_spmd.sunk | while | flops 164573184 | bytes 4859533 | solution.py:31
  61.9 3.2 fusion.117
  115.4 3.2 fusion.117
  147.4 3.2 fusion.117
  158.1 3.2 fusion.117
  179.4 3.2 fusion.117
  185.0 7.3 %all-to-all-start = ((bf16[64,8,1024]{2,0,1:T(8,128)(2,1)}), bf16[64,8,1024]{2,0,1:T(8,128)(2,1)S(1)}, u32[]{:S(2)}, u32[]{:S(2)}) async-start(bf16[64,8,1024]{2,0,1:T(8,128)(2,1)} %copy.36), calls=%async_computation | async-start | bytes 2097152 | tf_op jit(solution)/shard_map/all_to_all | solution.py:96
  192.4 25.7 %all-to-all-done = bf16[64,8,1024]{2,0,1:T(8,128)(2,1)S(1)} async-done(((bf16[64,8,1024]{2,0,1:T(8,128)(2,1)}), bf16[64,8,1024]{2,0,1:T(8,128)(2,1)S(1)}, u32[]{:S(2)}, u32[]{:S(2)}) %all-to-all-start) | async-done | bytes 1048608 | tf_op jit(solution)/shard_map/all_to_all | solution.py:96
  230.5 4.3 all-to-all-start.1
  237.3 4.4 all-reduce.7
  241.7 19.0 %all-reduce.4.cloned.1.call-done = f32[1,32,512]{2,1,0:T(8,128)} async-done(((f32[1,32,512]{2,1,0:T(8,128)}), f32[1,32,512]{2,1,0:T(8,128)}) %all-reduce.4.cloned.1.call-update) | async-done | bytes 65552 | tf_op jit(solution)/shard_map/psum | solution.py:115
  262.1 18.8 %all-reduce.6.cloned.1.call-done = f32[1,32,1024]{2,1,0:T(8,128)} async-done(((f32[1,32,1024]{2,1,0:T(8,128)}), f32[1,32,1024]{2,1,0:T(8,128)}) %all-reduce.6.cloned.1.call-update) | async-done | bytes 131088 | tf_op jit(solution)/shard_map/psum | solution.py:114
  282.4 4.3 reshape.145
  287.7 4.5 broadcast.105
  292.2 191.9 %while.27 = (s32[]{:T(128)}, bf16[16,4,64,1024]{3,2,1,0:T(8,128)(2,1)}, f32[16,4,1,1024]{3,1,2,0:T(4,128)}, bf16[16,4,8,1024]{3,2,1,0:T(8,128)(2,1)S(1)}, bf16[2...) while((s32[]{:T(128)}, ...), condition=%wide.region_8.9_spmd, body=%wide.region_5.8_spmd.sunk | while | flops 299106304 | bytes 13950577 | solution.py:31
  292.2 3.8 fusion.125
  295.9 5.2 %fusion.126 = (f32[4,1024]{1,0:T(4,128)S(1)}, f32[4,1024]{1,0:T(4,128)S(1)}, f32[4,64,1024]{2,1,0:T(8,128)S(1)}) fusion(f32[16,4,64,1024]{3,2,1,0:T(8,128)} %get-tuple-element.409, s32[]{:T(128)} %get-tuple-element.389, f32[64]{0:T(128)S(1)} %get-tuple-element.408, bf16[64,256]{1,0:T(8,128)(2,1)S(1)} %get-tuple-element.406, ...), kind=kOutput, calls=%fused_computation.108.clone.1 | convolution fusion | flops 163569664 | bytes 6429184 | tf_op jit(solution)/shard_map/while/body/eval_jaxpr/rfk,cf->rck/dot_general | solution.py:84
  304.2 3.8 fusion.125
  307.9 5.2 %fusion.126 = (f32[4,1024]{1,0:T(4,128)S(1)}, f32[4,1024]{1,0:T(4,128)S(1)}, f32[4,64,1024]{2,1,0:T(8,128)S(1)}) fusion(f32[16,4,64,1024]{3,2,1,0:T(8,128)} %get-tuple-element.409, s32[]{:T(128)} %get-tuple-element.389, f32[64]{0:T(128)S(1)} %get-tuple-element.408, bf16[64,256]{1,0:T(8,128)(2,1)S(1)} %get-tuple-element.406, ...), kind=kOutput, calls=%fused_computation.108.clone.1 | convolution fusion | flops 163569664 | bytes 6429184 | tf_op jit(solution)/shard_map/while/body/eval_jaxpr/rfk,cf->rck/dot_general | solution.py:84
  316.2 3.8 fusion.125
  319.9 5.2 %fusion.126 = (f32[4,1024]{1,0:T(4,128)S(1)}, f32[4,1024]{1,0:T(4,128)S(1)}, f32[4,64,1024]{2,1,0:T(8,128)S(1)}) fusion(f32[16,4,64,1024]{3,2,1,0:T(8,128)} %get-tuple-element.409, s32[]{:T(128)} %get-tuple-element.389, f32[64]{0:T(128)S(1)} %get-tuple-element.408, bf16[64,256]{1,0:T(8,128)(2,1)S(1)} %get-tuple-element.406, ...), kind=kOutput, calls=%fused_computation.108.clone.1 | convolution fusion | flops 163569664 | bytes 6429184 | tf_op jit(solution)/shard_map/while/body/eval_jaxpr/rfk,cf->rck/dot_general | solution.py:84
  328.2 3.8 fusion.125
  331.9 5.2 %fusion.126 = (f32[4,1024]{1,0:T(4,128)S(1)}, f32[4,1024]{1,0:T(4,128)S(1)}, f32[4,64,1024]{2,1,0:T(8,128)S(1)}) fusion(f32[16,4,64,1024]{3,2,1,0:T(8,128)} %get-tuple-element.409, s32[]{:T(128)} %get-tuple-element.389, f32[64]{0:T(128)S(1)} %get-tuple-element.408, bf16[64,256]{1,0:T(8,128)(2,1)S(1)} %get-tuple-element.406, ...), kind=kOutput, calls=%fused_computation.108.clone.1 | convolution fusion | flops 163569664 | bytes 6429184 | tf_op jit(solution)/shard_map/while/body/eval_jaxpr/rfk,cf->rck/dot_general | solution.py:84
  340.2 3.8 fusion.125
  343.9 5.2 %fusion.126 = (f32[4,1024]{1,0:T(4,128)S(1)}, f32[4,1024]{1,0:T(4,128)S(1)}, f32[4,64,1024]{2,1,0:T(8,128)S(1)}) fusion(f32[16,4,64,1024]{3,2,1,0:T(8,128)} %get-tuple-element.409, s32[]{:T(128)} %get-tuple-element.389, f32[64]{0:T(128)S(1)} %get-tuple-element.408, bf16[64,256]{1,0:T(8,128)(2,1)S(1)} %get-tuple-element.406, ...), kind=kOutput, calls=%fused_computation.108.clone.1 | convolution fusion | flops 163569664 | bytes 6429184 | tf_op jit(solution)/shard_map/while/body/eval_jaxpr/rfk,cf->rck/dot_general | solution.py:84
  352.2 3.8 fusion.125
  355.9 5.2 %fusion.126 = (f32[4,1024]{1,0:T(4,128)S(1)}, f32[4,1024]{1,0:T(4,128)S(1)}, f32[4,64,1024]{2,1,0:T(8,128)S(1)}) fusion(f32[16,4,64,1024]{3,2,1,0:T(8,128)} %get-tuple-element.409, s32[]{:T(128)} %get-tuple-element.389, f32[64]{0:T(128)S(1)} %get-tuple-element.408, bf16[64,256]{1,0:T(8,128)(2,1)S(1)} %get-tuple-element.406, ...), kind=kOutput, calls=%fused_computation.108.clone.1 | convolution fusion | flops 163569664 | bytes 6429184 | tf_op jit(solution)/shard_map/while/body/eval_jaxpr/rfk,cf->rck/dot_general | solution.py:84
  364.2 3.8 fusion.125
  367.9 5.2 %fusion.126 = (f32[4,1024]{1,0:T(4,128)S(1)}, f32[4,1024]{1,0:T(4,128)S(1)}, f32[4,64,1024]{2,1,0:T(8,128)S(1)}) fusion(f32[16,4,64,1024]{3,2,1,0:T(8,128)} %get-tuple-element.409, s32[]{:T(128)} %get-tuple-element.389, f32[64]{0:T(128)S(1)} %get-tuple-element.408, bf16[64,256]{1,0:T(8,128)(2,1)S(1)} %get-tuple-element.406, ...), kind=kOutput, calls=%fused_computation.108.clone.1 | convolution fusion | flops 163569664 | bytes 6429184 | tf_op jit(solution)/shard_map/while/body/eval_jaxpr/rfk,cf->rck/dot_general | solution.py:84
  376.2 3.8 fusion.125
  379.9 5.2 %fusion.126 = (f32[4,1024]{1,0:T(4,128)S(1)}, f32[4,1024]{1,0:T(4,128)S(1)}, f32[4,64,1024]{2,1,0:T(8,128)S(1)}) fusion(f32[16,4,64,1024]{3,2,1,0:T(8,128)} %get-tuple-element.409, s32[]{:T(128)} %get-tuple-element.389, f32[64]{0:T(128)S(1)} %get-tuple-element.408, bf16[64,256]{1,0:T(8,128)(2,1)S(1)} %get-tuple-element.406, ...), kind=kOutput, calls=%fused_computation.108.clone.1 | convolution fusion | flops 163569664 | bytes 6429184 | tf_op jit(solution)/shard_map/while/body/eval_jaxpr/rfk,cf->rck/dot_general | solution.py:84
  388.2 3.8 fusion.125
  391.9 5.2 %fusion.126 = (f32[4,1024]{1,0:T(4,128)S(1)}, f32[4,1024]{1,0:T(4,128)S(1)}, f32[4,64,1024]{2,1,0:T(8,128)S(1)}) fusion(f32[16,4,64,1024]{3,2,1,0:T(8,128)} %get-tuple-element.409, s32[]{:T(128)} %get-tuple-element.389, f32[64]{0:T(128)S(1)} %get-tuple-element.408, bf16[64,256]{1,0:T(8,128)(2,1)S(1)} %get-tuple-element.406, ...), kind=kOutput, calls=%fused_computation.108.clone.1 | convolution fusion | flops 163569664 | bytes 6429184 | tf_op jit(solution)/shard_map/while/body/eval_jaxpr/rfk,cf->rck/dot_general | solution.py:84
  400.2 3.8 fusion.125
  403.9 5.2 %fusion.126 = (f32[4,1024]{1,0:T(4,128)S(1)}, f32[4,1024]{1,0:T(4,128)S(1)}, f32[4,64,1024]{2,1,0:T(8,128)S(1)}) fusion(f32[16,4,64,1024]{3,2,1,0:T(8,128)} %get-tuple-element.409, s32[]{:T(128)} %get-tuple-element.389, f32[64]{0:T(128)S(1)} %get-tuple-element.408, bf16[64,256]{1,0:T(8,128)(2,1)S(1)} %get-tuple-element.406, ...), kind=kOutput, calls=%fused_computation.108.clone.1 | convolution fusion | flops 163569664 | bytes 6429184 | tf_op jit(solution)/shard_map/while/body/eval_jaxpr/rfk,cf->rck/dot_general | solution.py:84
  412.2 3.8 fusion.125
  415.9 5.2 %fusion.126 = (f32[4,1024]{1,0:T(4,128)S(1)}, f32[4,1024]{1,0:T(4,128)S(1)}, f32[4,64,1024]{2,1,0:T(8,128)S(1)}) fusion(f32[16,4,64,1024]{3,2,1,0:T(8,128)} %get-tuple-element.409, s32[]{:T(128)} %get-tuple-element.389, f32[64]{0:T(128)S(1)} %get-tuple-element.408, bf16[64,256]{1,0:T(8,128)(2,1)S(1)} %get-tuple-element.406, ...), kind=kOutput, calls=%fused_computation.108.clone.1 | convolution fusion | flops 163569664 | bytes 6429184 | tf_op jit(solution)/shard_map/while/body/eval_jaxpr/rfk,cf->rck/dot_general | solution.py:84
  424.2 3.8 fusion.125
  427.9 5.2 %fusion.126 = (f32[4,1024]{1,0:T(4,128)S(1)}, f32[4,1024]{1,0:T(4,128)S(1)}, f32[4,64,1024]{2,1,0:T(8,128)S(1)}) fusion(f32[16,4,64,1024]{3,2,1,0:T(8,128)} %get-tuple-element.409, s32[]{:T(128)} %get-tuple-element.389, f32[64]{0:T(128)S(1)} %get-tuple-element.408, bf16[64,256]{1,0:T(8,128)(2,1)S(1)} %get-tuple-element.406, ...), kind=kOutput, calls=%fused_computation.108.clone.1 | convolution fusion | flops 163569664 | bytes 6429184 | tf_op jit(solution)/shard_map/while/body/eval_jaxpr/rfk,cf->rck/dot_general | solution.py:84
  436.2 3.8 fusion.125
  439.9 5.2 %fusion.126 = (f32[4,1024]{1,0:T(4,128)S(1)}, f32[4,1024]{1,0:T(4,128)S(1)}, f32[4,64,1024]{2,1,0:T(8,128)S(1)}) fusion(f32[16,4,64,1024]{3,2,1,0:T(8,128)} %get-tuple-element.409, s32[]{:T(128)} %get-tuple-element.389, f32[64]{0:T(128)S(1)} %get-tuple-element.408, bf16[64,256]{1,0:T(8,128)(2,1)S(1)} %get-tuple-element.406, ...), kind=kOutput, calls=%fused_computation.108.clone.1 | convolution fusion | flops 163569664 | bytes 6429184 | tf_op jit(solution)/shard_map/while/body/eval_jaxpr/rfk,cf->rck/dot_general | solution.py:84
  448.2 3.8 fusion.125
  451.9 5.2 %fusion.126 = (f32[4,1024]{1,0:T(4,128)S(1)}, f32[4,1024]{1,0:T(4,128)S(1)}, f32[4,64,1024]{2,1,0:T(8,128)S(1)}) fusion(f32[16,4,64,1024]{3,2,1,0:T(8,128)} %get-tuple-element.409, s32[]{:T(128)} %get-tuple-element.389, f32[64]{0:T(128)S(1)} %get-tuple-element.408, bf16[64,256]{1,0:T(8,128)(2,1)S(1)} %get-tuple-element.406, ...), kind=kOutput, calls=%fused_computation.108.clone.1 | convolution fusion | flops 163569664 | bytes 6429184 | tf_op jit(solution)/shard_map/while/body/eval_jaxpr/rfk,cf->rck/dot_general | solution.py:84
  460.1 3.8 fusion.125
  463.9 5.2 %fusion.126 = (f32[4,1024]{1,0:T(4,128)S(1)}, f32[4,1024]{1,0:T(4,128)S(1)}, f32[4,64,1024]{2,1,0:T(8,128)S(1)}) fusion(f32[16,4,64,1024]{3,2,1,0:T(8,128)} %get-tuple-element.409, s32[]{:T(128)} %get-tuple-element.389, f32[64]{0:T(128)S(1)} %get-tuple-element.408, bf16[64,256]{1,0:T(8,128)(2,1)S(1)} %get-tuple-element.406, ...), kind=kOutput, calls=%fused_computation.108.clone.1 | convolution fusion | flops 163569664 | bytes 6429184 | tf_op jit(solution)/shard_map/while/body/eval_jaxpr/rfk,cf->rck/dot_general | solution.py:84
  472.1 3.8 fusion.125
  475.9 5.2 %fusion.126 = (f32[4,1024]{1,0:T(4,128)S(1)}, f32[4,1024]{1,0:T(4,128)S(1)}, f32[4,64,1024]{2,1,0:T(8,128)S(1)}) fusion(f32[16,4,64,1024]{3,2,1,0:T(8,128)} %get-tuple-element.409, s32[]{:T(128)} %get-tuple-element.389, f32[64]{0:T(128)S(1)} %get-tuple-element.408, bf16[64,256]{1,0:T(8,128)(2,1)S(1)} %get-tuple-element.406, ...), kind=kOutput, calls=%fused_computation.108.clone.1 | convolution fusion | flops 163569664 | bytes 6429184 | tf_op jit(solution)/shard_map/while/body/eval_jaxpr/rfk,cf->rck/dot_general | solution.py:84
  (256 shorter events, 224.7 us)
Async XLA Ops:
  7.2 213.0 %copy-start = (bf16[1,32,1024]{2,1,0:T(8,128)(2,1)S(1)}, bf16[1,32,1024]{2,1,0:T(8,128)(2,1)}, u32[]{:S(2)}) copy-start(bf16[1,32,1024]{2,1,0:T(8,128)(2,1)} %param.27) | copy-start | bytes 196612
  8.2 4.4 copy-start.2
  8.3 4.3 copy-start.6
  8.3 4.3 copy-start.8
  8.3 4.3 copy-start.11
  8.3 4.3 copy-start.12
  183.5 8.9 %copy-start.3 = (bf16[1,32,512]{2,1,0:T(8,128)(2,1)S(1)}, bf16[1,32,512]{2,1,0:T(8,128)(2,1)}, u32[]{:S(2)}) copy-start(bf16[1,32,512]{2,1,0:T(8,128)(2,1)} %param.30) | copy-start | bytes 98308
  183.5 8.9 %copy-start.7 = (bf16[1,32,512]{2,1,0:T(8,128)(2,1)S(1)}, bf16[1,32,512]{2,1,0:T(8,128)(2,1)}, u32[]{:S(2)}) copy-start(bf16[1,32,512]{2,1,0:T(8,128)(2,1)} %param.29) | copy-start | bytes 98308
  183.5 8.9 %copy-start.9 = (s32[1024]{0:T(1024)S(1)}, s32[1024]{0:T(1024)}, u32[]{:S(2)}) copy-start(s32[1024]{0:T(1024)} %param.25) | copy-start | bytes 12292
  185.0 33.1 %all-to-all-start = ((bf16[64,8,1024]{2,0,1:T(8,128)(2,1)}), bf16[64,8,1024]{2,0,1:T(8,128)(2,1)S(1)}, u32[]{:S(2)}, u32[]{:S(2)}) async-start(bf16[64,8,1024]{2,0,1:T(8,128)(2,1)} %copy.36), calls=%async_computation | async-start | bytes 2097152 | tf_op jit(solution)/shard_map/all_to_all | solution.py:96
  192.4 27.8 %copy-start.4 = (bf16[1,32,512]{2,1,0:T(8,128)(2,1)S(1)}, bf16[1,32,512]{2,1,0:T(8,128)(2,1)}, u32[]{:S(2)}) copy-start(bf16[1,32,512]{2,1,0:T(8,128)(2,1)} %param.26) | copy-start | bytes 98308
  192.4 27.8 %copy-start.10 = (f32[1,512]{1,0:T(1,128)S(1)}, f32[1,512]{1,0:T(1,128)}, u32[]{:S(2)}) copy-start(f32[1,512]{1,0:T(1,128)} %param.31) | copy-start | bytes 6148
  218.4 4.1 copy-start.5
  230.5 52.0 %all-to-all-start.1 = ((bf16[8,2,32768]{2,1,0:T(2,128)(2,1)}), bf16[8,2,32768]{2,1,0:T(2,128)(2,1)}, u32[]{:S(2)}, u32[]{:S(2)}) async-start(bf16[8,2,32768]{2,1,0:T(2,128)(2,1)} %reshape.144), calls=%async_computation.1 | async-start | bytes 2097152 | tf_op jit(solution)/shard_map/all_to_all | solution.py:107
  234.7 25.9 %all-reduce.4.cloned.1.call-start = ((), (), s32[]{:S(2)}) async-start(), calls=%async_computation.2 | async-start | bytes 131072 | tf_op jit(solution)/shard_map/psum | solution.py:115
  235.7 45.1 %all-reduce.6.cloned.1.call-start = ((), (), s32[]{:S(2)}) async-start(), calls=%async_computation.3 | async-start | bytes 262144 | tf_op jit(solution)/shard_map/psum | solution.py:114
  484.1 0.8 copy-start.1
Sparse Core Ops, SparseCore 0:
  238.4 22.2 all-reduce.3
  262.9 17.9 all-reduce.5
where the time goes:
time: 498 us; the launch traced here: 492 us
  matrix products  204 us (41%)
  other arithmetic  157 us (32%)
  waiting for transfers between devices  63.5 us (13%)
  local copies, waits for them, and re-layouts  36.4 us (7%)
  between operations  14.2 us (3%)
  starting transfers between devices  11.7 us (2%)
    dynamic_update_slice x64, other arithmetic, by_groups(): result = lax.map(lambda blocks: kernel_fn(*blocks), stacked)  113 us
    dot_general x16, matrix products, backward_rows(): jnp.einsum('rfk,cf->rck', dpre, w_in, preferred_element_type=jnp.float32)  83.7 us
    dot_general x16, matrix products, backward_rows(): jnp.einsum('rck,cf->rfk', normed, w_in, preferred_element_type=jnp.float32)  60.1 us
    dot_general x16, matrix products, forward_rows(): jnp.einsum('rfk,fh->rhk', hidden, w_out, preferred_element_type=jnp.float32)  51.3 us
    all_to_all x1, waiting for transfers between devices, per_device(): lax.all_to_all(bias_vals, 'heads', split_axis=1, concat_axis=0, tiled=True)  25.7 us
    reduce_sum x16, other arithmetic, normalize(): jnp.mean(centre * centre, axis=1, keepdims=True) + 1e-05  19.5 us
    psum x1, waiting for transfers between devices, per_device(): dq_sum = lax.psum(dq_total, 'key')  19 us
    psum x1, waiting for transfers between devices, per_device(): dk_sum, dv_sum = lax.psum((dk_cat, dv_cat), 'query')  18.8 us
  transfers between devices with their start and end apart: 4, of which 3 were waited for; matrix products, arithmetic and copies ran while one was open for 1% of the time, Pallas kernels for 0%

commit v1 on v0

v1 whole, which is shorter than its diff:
```python
import functools
import math

import jax
import jax.numpy as jnp
from jax import lax
from jax.experimental import pallas as pl
from jax.experimental.pallas import tpu as pltpu
from jax.sharding import PartitionSpec as P

F32 = jnp.float32
BF16 = jnp.bfloat16
RSQRT2 = 1.0 / math.sqrt(2.0)
EXP2_SCALE = -0.5 / math.log(2.0)
EXP2_SHIFT = math.log2(2.0 / math.sqrt(2.0 * math.pi))
PAD = 16
VMEM_LIMIT = 60 << 20


def full_spec(array):
    return pl.BlockSpec(array.shape, lambda *_: (0,) * array.ndim)


def divisor(total, largest):
    return math.gcd(total, largest)


def split_three(values):
    high = lax.reduce_precision(values, 8, 7)
    mid = lax.reduce_precision(values - high, 8, 7)
    low = lax.reduce_precision(values - high - mid, 8, 7)
    return [piece.astype(BF16) for piece in (high, mid, low)]


def axis_sum(values, name):
    if lax.axis_size(name) == 2:
        return values + lax.ppermute(values, name, [(0, 1), (1, 0)])
    return lax.psum(values, name)


def unit_norm(values):
    centre = values - jnp.mean(values, axis=0, keepdims=True)
    inv_std = lax.rsqrt(jnp.mean(centre * centre, axis=0, keepdims=True) + 1e-05)
    return centre * inv_std, inv_std


def forward_kernel(
    pair_ref, bucket_ref, w_pre_ref, w_mix_ref, table_ref, gain_ref, slope_ref, bias_ref, *, group, tile
):
    rows, chans, keys = pair_ref.shape
    heads = w_mix_ref.shape[0]
    extra = w_pre_ref.shape[1] - chans
    buckets = table_ref.shape[1]
    key_tiles = keys // tile
    ones = jnp.where(lax.broadcasted_iota(jnp.int32, (extra, tile), 0) < 3, 1.0, 0.0).astype(BF16)

    def one_row(row, cols):
        unit_pairs, _ = unit_norm(pair_ref[row, :, cols].astype(F32))
        normed = (unit_pairs * gain_ref[...]).astype(BF16)
        pre_act = jnp.dot(
            w_pre_ref[...], jnp.concatenate([normed, ones], axis=0), preferred_element_type=F32
        )
        cdf2 = lax.erf(pre_act * RSQRT2) + 1.0
        hidden2 = (pre_act * cdf2).astype(BF16)
        density2 = jnp.exp2(pre_act * pre_act * EXP2_SCALE + EXP2_SHIFT)
        slope_ref[row, :, cols] = (cdf2 + pre_act * density2).astype(BF16)
        bucket_iota = lax.broadcasted_iota(jnp.int32, (buckets, tile), 0)
        onehot = jnp.where(bucket_ref[row, :, cols] == bucket_iota, 1.0, 0.0).astype(BF16)
        mixed = jnp.dot(w_mix_ref[...], hidden2, preferred_element_type=F32)
        return mixed + jnp.dot(table_ref[...], onehot, preferred_element_type=F32)

    def step(index, carry):
        row_group = index // key_tiles
        cols = pl.ds(pl.multiple_of((index % key_tiles) * tile, tile), tile)
        outs = [one_row(row_group * group + member, cols) for member in range(group)]
        size = group * heads
        bias_ref[pl.ds(pl.multiple_of(row_group * size, size), size), cols] = jnp.concatenate(
            outs, axis=0
        ).astype(BF16)
        return carry

    lax.fori_loop(0, (rows // group) * key_tiles, step, 0)


def forward_call(pair_feats, bucket_ids, w_pre, w_mix, table, gain):
    rows, chans, keys = pair_feats.shape
    hid = w_pre.shape[0]
    heads = w_mix.shape[0]
    block = divisor(rows, 4)
    group = divisor(block, 4)
    tile = divisor(keys, 512)
    return pl.pallas_call(
        functools.partial(forward_kernel, group=group, tile=tile),
        grid=(rows // block,),
        in_specs=[
            pl.BlockSpec((block, chans, keys), lambda i: (i, 0, 0)),
            pl.BlockSpec((block, 1, keys), lambda i: (i, 0, 0)),
            full_spec(w_pre),
            full_spec(w_mix),
            full_spec(table),
            full_spec(gain),
        ],
        out_specs=[
            pl.BlockSpec((block, hid, keys), lambda i: (i, 0, 0)),
            pl.BlockSpec((block * heads, keys), lambda i: (i, 0)),
        ],
        out_shape=[
            jax.ShapeDtypeStruct((rows, hid, keys), BF16),
            jax.ShapeDtypeStruct((rows * heads, keys), BF16),
        ],
        compiler_params=pltpu.CompilerParams(vmem_limit_bytes=VMEM_LIMIT),
        cost_estimate=pl.CostEstimate(
            flops=2 * rows * keys * hid * 256,
            bytes_accessed=2 * rows * keys * (hid + chans),
            transcendentals=2 * rows * keys * hid,
        ),
        name="pair_forward",
    )(pair_feats, bucket_ids[:, None, :], w_pre, w_mix, table, gain)


def attention_kernel(
    bias_ref, kv_ref, qd_ref, mask_ref, ds_ref, dkv_ref, dq_ref, q_rows, d_rows, q_cols, d_cols, norm_ref,
    delta_ref, dq_acc, *, head_dim
):
    heads, _, rows = qd_ref.shape
    tile = bias_ref.shape[1]
    width = heads * head_dim
    flat = rows * heads
    scale = 1.0 / math.sqrt(head_dim)
    nt = (((1,), (1,)), ((), ()))
    step = pl.program_id(0)
    expand = (
        lax.broadcasted_iota(jnp.int32, (flat, rows), 0) // heads
        == lax.broadcasted_iota(jnp.int32, (flat, rows), 1)
    )

    @pl.when(step == 0)
    def _():
        expand_low = jnp.where(expand, 1.0, 0.0).astype(BF16)
        own_rows = (
            lax.broadcasted_iota(jnp.int32, (flat, width), 0) % heads
            == lax.broadcasted_iota(jnp.int32, (flat, width), 1) // head_dim
        )
        own_cols = (
            lax.broadcasted_iota(jnp.int32, (width, flat), 1) % heads
            == lax.broadcasted_iota(jnp.int32, (width, flat), 0) // head_dim
        )
        for begin, by_rows, by_cols in ((0, q_rows, q_cols), (head_dim, d_rows, d_cols)):
            block = qd_ref[:, begin : begin + head_dim, :].reshape(width, rows)
            spread = lax.dot_general(expand_low, block, nt, preferred_element_type=F32)
            by_rows[...] = jnp.where(own_rows, spread, 0.0).astype(BF16)
            spread = lax.dot_general(block, expand_low, nt, preferred_element_type=F32)
            by_cols[...] = jnp.where(own_cols, spread, 0.0).astype(BF16)
        tail = qd_ref[:, 2 * head_dim :, :].astype(F32)
        lane = lax.broadcasted_iota(jnp.int32, (rows, heads, rows), 2)
        own_lane = lane == lax.broadcasted_iota(jnp.int32, (rows, heads, rows), 0)
        for begin, target in ((0, norm_ref), (3, delta_ref)):
            pieces = tail[:, begin, :] + tail[:, begin + 1, :] + tail[:, begin + 2, :]
            column = jnp.sum(jnp.where(own_lane, pieces[None], 0.0), axis=2, keepdims=True)
            target[...] = jnp.broadcast_to(column.reshape(flat, 1), target.shape)
        dq_acc[...] = jnp.zeros_like(dq_acc)

    copies = tile // norm_ref.shape[1]
    norm = jnp.concatenate([norm_ref[...]] * copies, axis=1)
    delta = jnp.concatenate([delta_ref[...]] * copies, axis=1)
    keys = kv_ref[:, :head_dim, :].reshape(width, tile)
    values = kv_ref[:, head_dim:, :].reshape(width, tile)
    scores = jnp.dot(q_rows[...], keys, preferred_element_type=F32) * scale + bias_ref[...].astype(F32)
    probs = jnp.where(mask_ref[...] == 1, jnp.exp(scores - norm), 0.0)
    dprobs = jnp.dot(d_rows[...], values, preferred_element_type=F32)
    dscores = (probs * (dprobs - delta)).astype(BF16)
    ds_ref[...] = dscores
    dk_part = jnp.dot(q_cols[...], dscores, preferred_element_type=F32)
    dv_part = jnp.dot(d_cols[...], probs.astype(BF16), preferred_element_type=F32)
    dkv_ref[:, :head_dim, :] = dk_part.reshape(heads, head_dim, tile).astype(dkv_ref.dtype)
    dkv_ref[:, head_dim:, :] = dv_part.reshape(heads, head_dim, tile).astype(dkv_ref.dtype)
    dq_acc[...] += lax.dot_general(keys, dscores, nt, preferred_element_type=F32)

    @pl.when(step == pl.num_programs(0) - 1)
    def _():
        own_cols = (
            lax.broadcasted_iota(jnp.int32, (width, flat), 1) % heads
            == lax.broadcasted_iota(jnp.int32, (width, flat), 0) // head_dim
        )
        mine = jnp.where(own_cols, dq_acc[...], 0.0)
        total = jnp.dot(
            mine, jnp.where(expand, 1.0, 0.0), precision=lax.Precision.HIGHEST, preferred_element_type=F32
        )
        dq_ref[...] = total.reshape(heads, head_dim, rows)


def attention_call(bias, kv, qd, key_mask, head_dim):
    flat, keys = bias.shape
    heads, depth, rows = qd.shape
    width = heads * head_dim
    tile = divisor(keys, 256)
    lanes = divisor(tile, 128)
    return pl.pallas_call(
        functools.partial(attention_kernel, head_dim=head_dim),
        grid=(keys // tile,),
        in_specs=[
            pl.BlockSpec((flat, tile), lambda i: (0, i)),
            pl.BlockSpec((heads, 2 * head_dim, tile), lambda i: (0, 0, i)),
            full_spec(qd),
            pl.BlockSpec((1, tile), lambda i: (0, i)),
        ],
        out_specs=[
            pl.BlockSpec((flat, tile), lambda i: (0, i)),
            pl.BlockSpec((heads, 2 * head_dim, tile), lambda i: (0, 0, i)),
            pl.BlockSpec((heads, head_dim, rows), lambda i: (0, 0, 0)),
        ],
        out_shape=[
            jax.ShapeDtypeStruct((flat, keys), BF16),
            jax.ShapeDtypeStruct((heads, 2 * head_dim, keys), BF16),
            jax.ShapeDtypeStruct((heads, head_dim, rows), F32),
        ],
        scratch_shapes=[
            pltpu.VMEM((flat, width), BF16),
            pltpu.VMEM((flat, width), BF16),
            pltpu.VMEM((width, flat), BF16),
            pltpu.VMEM((width, flat), BF16),
            pltpu.VMEM((flat, lanes), F32),
            pltpu.VMEM((flat, lanes), F32),
            pltpu.VMEM((width, flat), F32),
        ],
        compiler_params=pltpu.CompilerParams(vmem_limit_bytes=VMEM_LIMIT),
        cost_estimate=pl.CostEstimate(
            flops=10 * flat * keys * width, bytes_accessed=8 * flat * keys, transcendentals=flat * keys
        ),
        name="pair_attention",
    )(bias, kv, qd, key_mask.reshape(1, keys))


def backward_kernel(pair_ref, ds_ref, slope_ref, w_back_ref, w_in_ref, gain_ref, out_ref, *, group, tile):
    rows, chans, keys = pair_ref.shape
    heads = w_back_ref.shape[1]
    key_tiles = keys // tile

    def step(index, carry):
        row_group = index // key_tiles
        cols = pl.ds(pl.multiple_of((index % key_tiles) * tile, tile), tile)
        size = group * heads
        dscores = ds_ref[pl.ds(pl.multiple_of(row_group * size, size), size), cols]
        for member in range(group):
            row = row_group * group + member
            unit_pairs, inv_std = unit_norm(pair_ref[row, :, cols].astype(F32))
            dhidden = jnp.dot(
                w_back_ref[...], dscores[member * heads : (member + 1) * heads], preferred_element_type=F32
            )
            dpre = (dhidden * slope_ref[row, :, cols].astype(F32)).astype(BF16)
            dunit = jnp.dot(w_in_ref[...], dpre, preferred_element_type=F32) * gain_ref[...]
            first_mean = jnp.mean(dunit, axis=0, keepdims=True)
            second_mean = jnp.mean(dunit * unit_pairs, axis=0, keepdims=True)
            grad = inv_std * (dunit - first_mean - unit_pairs * second_mean)
            out_ref[row, :, cols] = grad.astype(BF16)
        return carry

    lax.fori_loop(0, (rows // group) * key_tiles, step, 0)


def backward_call(pair_feats, dscores, slope, w_back, w_in, gain):
    rows, chans, keys = pair_feats.shape
    hid, heads = w_back.shape
    block = divisor(rows, 4)
    group = divisor(block, 4)
    tile = divisor(keys, 512)
    return pl.pallas_call(
        functools.partial(backward_kernel, group=group, tile=tile),
        grid=(rows // block,),
        in_specs=[
            pl.BlockSpec((block, chans, keys), lambda i: (i, 0, 0)),
            pl.BlockSpec((block * heads, keys), lambda i: (i, 0)),
            pl.BlockSpec((block, hid, keys), lambda i: (i, 0, 0)),
            full_spec(w_back),
            full_spec(w_in),
            full_spec(gain),
        ],
        out_specs=pl.BlockSpec((block, chans, keys), lambda i: (i, 0, 0)),
        out_shape=jax.ShapeDtypeStruct((rows, chans, keys), BF16),
        compiler_params=pltpu.CompilerParams(vmem_limit_bytes=VMEM_LIMIT),
        cost_estimate=pl.CostEstimate(
            flops=2 * rows * keys * hid * 256,
            bytes_accessed=2 * rows * keys * (hid + 2 * chans),
            transcendentals=0,
        ),
        name="pair_backward",
    )(pair_feats, dscores, slope, w_back, w_in, gain)


def per_device(
    pair_feats,
    bucket_ids,
    ln_gain,
    w_in,
    b_in,
    w_out,
    bucket_table,
    key_mask,
    q_heads,
    k_heads,
    v_heads,
    out_heads,
    dout_heads,
    log_norm,
):
    axis_size = lax.axis_size("heads")
    own_heads, head_dim, queries = q_heads.shape
    keys = k_heads.shape[2]
    score_scale = 1.0 / math.sqrt(head_dim)

    kv = jnp.concatenate([k_heads, v_heads], axis=1)
    kv_all = lax.all_to_all(
        jnp.broadcast_to(kv[None], (axis_size,) + kv.shape), "heads", split_axis=0, concat_axis=0, tiled=True
    ).reshape(axis_size * own_heads, 2 * head_dim, keys)
    deltas = jnp.sum(dout_heads.astype(F32) * out_heads.astype(F32), axis=1)
    scalars = [piece[:, None, :] for piece in split_three(log_norm) + split_three(deltas)]
    fill = -(2 * head_dim + len(scalars)) % PAD
    packed = jnp.concatenate(
        [q_heads, dout_heads] + scalars + [jnp.zeros((own_heads, fill, queries), BF16)], axis=1
    )
    qd_all = lax.all_to_all(packed, "heads", split_axis=2, concat_axis=0, tiled=True)

    gain = ln_gain[:, None]
    bias_rows = [piece[:, None] for piece in split_three(b_in)]
    hid = b_in.shape[0]
    w_pre = jnp.concatenate([w_in.T] + bias_rows + [jnp.zeros((hid, PAD - 3), BF16)], axis=1)
    half_out = w_out * jnp.asarray(0.5, BF16)

    slope, bias_vals = forward_call(pair_feats, bucket_ids, w_pre, half_out.T, bucket_table.T, gain)
    dscores, dkv_part, dq_part = attention_call(bias_vals, kv_all, qd_all, key_mask, head_dim)
    dkv_all = lax.all_to_all(dkv_part, "heads", split_axis=0, concat_axis=0, tiled=True)
    dq_all = lax.all_to_all(dq_part, "heads", split_axis=0, concat_axis=2, tiled=True)
    grad_pairs = backward_call(pair_feats, dscores, slope, half_out, w_in, gain)

    dkv_sum = jnp.sum(
        dkv_all.reshape(axis_size, own_heads, 2 * head_dim, keys).astype(F32), axis=0
    )
    dkv_sum = axis_sum(dkv_sum, "query")
    dq_sum = axis_sum(dq_all, "key")
    grad_q = (dq_sum * score_scale).astype(BF16)
    grad_k = (dkv_sum[:, :head_dim] * score_scale).astype(BF16)
    grad_v = dkv_sum[:, head_dim:].astype(BF16)
    return (grad_pairs, grad_q, grad_k, grad_v)


def solution(mesh):
    def traced(*args):
        with jax.sharding.use_abstract_mesh(mesh.abstract_mesh):
            return jax.shard_map(
                per_device,
                mesh=mesh,
                in_specs=(
                    P(("query", "heads"), None, "key"),
                    P(("query", "heads"), "key"),
                    P(),
                    P(),
                    P(),
                    P(),
                    P(),
                    P("key"),
                    P("heads", None, "query"),
                    P("heads", None, "key"),
                    P("heads", None, "key"),
                    P("heads", None, "query"),
                    P("heads", None, "query"),
                    P("heads", "query"),
                ),
                out_specs=(
                    P(("query", "heads"), None, "key"),
                    P("heads", None, "query"),
                    P("heads", None, "key"),
                    P("heads", None, "key"),
                ),
                check_vma=False,
            )(*args)

    return traced
```

time: 498 us -> 173 us (0.35)
  matrix products: 204 us -> 0 us
  other arithmetic: 157 us -> 7.42 us
  Pallas kernels: 0 us -> 93.3 us
  waiting for transfers between devices: 63.5 us -> 26 us
  local copies, waits for them, and re-layouts: 36.4 us -> 15.5 us
  between operations: 14.2 us -> 0.78 us
  blocking collectives: 4.36 us -> 12.6 us
    dot_general x69 -> x0, matrix products: 204 us -> none  [the longest x16 83.7 us: backward_rows(): jnp.einsum('rfk,cf->rck', dpre, w_in, preferred_element_type=jnp.float32)]
    dynamic_update_slice x64 -> x0, other arithmetic: 113 us -> none  [by_groups(): result = lax.map(lambda blocks: kernel_fn(*blocks), stacked)]
    pallas_call x0 -> x3, Pallas kernels: none -> 93.3 us  [the longest x1 49.9 us: forward_call(): pl.pallas_call(functools.partial(forward_kernel, group=group, tile=tile),...]
    psum x2 -> x0, waiting for transfers between devices: 37.7 us -> none  [the longest x1 19 us: per_device(): dq_sum = lax.psum(dq_total, 'key')]
    reduce_sum x33 -> x2, other arithmetic: 37.9 us -> 0.97 us  [the longest x1 0.8 us: per_device(): deltas = jnp.sum(dout_heads.astype(F32) * out_heads.astype(F32), axis=1)]
    all_to_all x0 -> x1, blocking collectives: none -> 12.6 us  [per_device(): lax.all_to_all(dq_part, 'heads', split_axis=0, concat_axis=2, tiled=True)]
    mul x16 -> x0, local copies, waits for them, and re-layouts: 11.6 us -> none  [backward_rows(): inv_std * (dunit - first_mean - unit_pairs * second_mean)]
    another operation x2 -> x0, local copies, waits for them, and re-layouts: 8.76 us -> none
  transfers between devices with their start and end apart: 4 -> 5, of which waited for: 3 -> 2; matrix products, arithmetic and copies ran while one was open for 1% -> 7% of each run, Pallas kernels for 0% -> 51%
where the time goes in v1:
time: 173 us; the launch traced here: 172 us
  Pallas kernels  93.3 us (54%)
  waiting for transfers between devices  26 us (15%)
  starting transfers between devices  16 us (9%)
  local copies, waits for them, and re-layouts  15.5 us (9%)
  blocking collectives  12.6 us (7%)
  other arithmetic  7.42 us (4%)
    pallas_call x1, Pallas kernels, forward_call(): pl.pallas_call(functools.partial(forward_kernel, group=group, tile=tile),...  49.9 us
    pallas_call x1, Pallas kernels, backward_call(): pl.pallas_call(functools.partial(backward_kernel, group=group, tile=tile)...  36.9 us
    all_to_all x1, waiting for transfers between devices, per_device(): lax.all_to_all(dkv_part, 'heads', split_axis=0, concat_axis=0, tiled=True)  19.9 us
    all_to_all x1, blocking collectives, per_device(): lax.all_to_all(dq_part, 'heads', split_axis=0, concat_axis=2, tiled=True)  12.6 us
    all_to_all x1, starting transfers between devices, per_device(): lax.all_to_all(packed, 'heads', split_axis=2, concat_axis=0, tiled=True)  7.31 us
    pallas_call x1, Pallas kernels, attention_call(): pl.pallas_call(functools.partial(attention_kernel, head_dim=head_dim), gr...  6.6 us
    all_to_all x1, waiting for transfers between devices, per_device(): lax.all_to_all(packed, 'heads', split_axis=2, concat_axis=0, tiled=True)  6.13 us
    unnamed x10, local copies, waits for them, and re-layouts  5.5 us
  transfers between devices with their start and end apart: 5, of which 2 were waited for; matrix products, arithmetic and copies ran while one was open for 7% of the time, Pallas kernels for 51%

profile of v1, /device:TPU:0, one launch (start us, length us, event | category | flops | bytes accessed | tf_op | source)
XLA Modules:
  0.0 171.7 jit_solution(4486227669923449898)
XLA Ops:
  0.6 0.8 multiply_reduce_fusion
  1.4 0.7 fusion.5
  2.1 1.7 concatenate.11
  3.8 0.2 copy.72
  4.0 0.5 broadcast.1
  4.5 1.4 reduce.3
  6.0 0.9 reshape.73
  6.9 7.3 %all-to-all-start.1 = ((bf16[8,2,2560]{2,1,0:T(2,128)(2,1)}), bf16[8,2,2560]{2,1,0:T(2,128)(2,1)S(1)}, u32[]{:S(2)}, u32[]{:S(2)}) async-start(bf16[8,2,2560]{2,1,0:T(2,128)(2,1)} %reshape.73), calls=%async_computation.1 | async-start | bytes 163840 | tf_op jit(solution)/shard_map/all_to_all | solution.py:321
  14.2 0.9 maximum_bitcast_fusion
  15.1 6.1 %all-to-all-done.1 = bf16[8,2,2560]{2,1,0:T(2,128)(2,1)S(1)} async-done(((bf16[8,2,2560]{2,1,0:T(2,128)(2,1)}), bf16[8,2,2560]{2,1,0:T(2,128)(2,1)S(1)}, u32[]{:S(2)}, u32[]{:S(2)}) %all-to-all-start.1) | async-done | bytes 81952 | tf_op jit(solution)/shard_map/all_to_all | solution.py:321
  21.2 1.1 broadcast_in_dim.48
  22.3 3.6 %all-to-all-start = ((bf16[8,1,64,1024]{3,2,1,0:T(8,128)(2,1)}), bf16[8,1,64,1024]{3,2,1,0:T(8,128)(2,1)S(1)}, u32[]{:S(2)}, u32[]{:S(2)}) async-start(bf16[8,1,64,1024]{3,2,1,0:T(8,128)(2,1)} %broadcast_in_dim.48), calls=%async_computation | async-start | bytes 2097152 | tf_op jit(solution)/shard_map/all_to_all | solution.py:312
  25.9 0.7 fusion.9
  26.5 0.1 broadcast_in_dim.53
  26.6 0.1 broadcast_in_dim.54
  26.7 0.1 broadcast_in_dim.55
  26.9 0.9 copy.65
  27.7 0.8 copy.69
  28.5 0.6 broadcast_multiply_fusion
  29.2 0.7 copy.70.w_mix_ref
  29.9 1.4 copy.71.gain_ref
  31.2 1.8 %broadcast_in_dim.41.bucket_ref = s32[64,1,1024]{2,1,0:T(1,128)} reshape(s32[64,1024]{1,0:T(8,128)} %param.15) | data formatting | bytes 524288 | tf_op jit(solution)/shard_map/broadcast_in_dim | solution.py:118
  33.1 0.8 concatenate.9.w_pre_ref
  33.9 49.9 %pair_forward.1 = (bf16[64,256,1024]{2,1,0:T(8,128)(2,1)}, bf16[512,1024]{1,0:T(8,128)(2,1)}) custom-call(bf16[64,64,1024]{2,1,0:T(8,128)(2,1)} %pair_ref.3, s32[64,1,1024]{2,1,0:T(1,128)} %broadcast_in_dim.41.bucket_ref, bf16[256,80]{1,0:T(8,128)(2,1)} %concatenate.9.w_pre_ref, bf16[8,256]{1,0:T(8,128)(2,1)} %copy.70.w_mix_ref, bf16[8,32]{1,0:T(8,128)(2,1)} %bitcast.40, ...), custom_call_target="tpu_custom_call" | custom-call | flops 8589934592 | bytes 41943040 | tf_op jit(solution)/shard_map/pair_forward/pallas_call | solution.py:92
  83.7 0.3 reshape.74
  84.0 0.8 copy.74
  84.8 0.0 all-to-all-done
  84.8 0.0 copy-start
  84.8 1.0 copy-done
  85.8 6.6 %pair_attention.1 = (bf16[512,1024]{1,0:T(8,128)(2,1)}, bf16[8,64,1024]{2,1,0:T(8,128)(2,1)}, f32[8,32,64]{2,1,0:T(8,128)}) custom-call(bf16[512,1024]{1,0:T(8,128)(2,1)} %get-tuple-element.9.bias_ref, bf16[8,64,1024]{2,1,0:T(8,128)(2,1)} %bitcast.30, bf16[8,80,64]{2,1,0:T(8,128)(2,1)} %bitcast.36, s32[1,1024]{1,0:T(1,128)} %bitcast.39), custom_call_target="tpu_custom_call" | custom-call | flops 1342177280 | bytes 4194304 | tf_op jit(solution)/shard_map/pair_attention/pallas_call | solution.py:198
  92.4 1.0 reshape.75
  93.5 12.6 %all_to_all.46 = f32[8,1,2048]{2,1,0:T(1,128)S(1)} all-to-all(f32[8,1,2048]{2,1,0:T(1,128)S(1)} %reshape.75), channel_id=1, replica_groups=mesh['query'=2,'key'=2,'heads'=8] {'heads'}, dimensions={0} | all-to-all | bytes 131072 | tf_op jit(solution)/shard_map/all_to_all | solution.py:332
  106.1 3.6 %all-to-all-start.3 = ((bf16[8,64,1024]{2,1,0:T(8,128)(2,1)}), bf16[8,64,1024]{2,1,0:T(8,128)(2,1)S(1)}, u32[]{:S(2)}, u32[]{:S(2)}) async-start(bf16[8,64,1024]{2,1,0:T(8,128)(2,1)} %get-tuple-element.13), calls=%async_computation.3 | async-start | bytes 2097152 | tf_op jit(solution)/shard_map/all_to_all | solution.py:331
  109.7 0.5 broadcast.2
  110.2 0.8 reduce.4
  111.0 0.1 reshape.76
  111.1 0.1 copy.76
  111.1 0.1 all_to_all.40
  111.2 1.6 collective-permute-start
  112.8 19.9 %all-to-all-done.3 = bf16[8,64,1024]{2,1,0:T(8,128)(2,1)S(1)} async-done(((bf16[8,64,1024]{2,1,0:T(8,128)(2,1)}), bf16[8,64,1024]{2,1,0:T(8,128)(2,1)S(1)}, u32[]{:S(2)}, u32[]{:S(2)}) %all-to-all-start.3) | async-done | bytes 1048608 | tf_op jit(solution)/shard_map/all_to_all | solution.py:331
  132.7 0.2 convert_reduce_fusion
  132.8 0.1 collective-permute-start.1
  132.9 36.9 %pair_backward.1 = bf16[64,64,1024]{2,1,0:T(8,128)(2,1)} custom-call(bf16[64,64,1024]{2,1,0:T(8,128)(2,1)} %pair_ref.3, bf16[512,1024]{1,0:T(8,128)(2,1)} %get-tuple-element.10.ds_ref, bf16[64,256,1024]{2,1,0:T(8,128)(2,1)} %get-tuple-element.11.slope_ref, bf16[256,8]{1,0:T(8,128)(2,1)} %get-tuple-element.14.w_back_ref, bf16[64,256]{1,0:T(8,128)(2,1)} %w_in_ref.1, ...), custom_call_target="tpu_custom_call" | custom-call | flops 8589934592 | bytes 50331648 | tf_op jit(solution)/shard_map/pair_backward/pallas_call | solution.py:267
  169.8 0.0 collective-permute-done
  169.8 0.6 multiply_convert_fusion
  170.4 0.0 collective-permute-done.1
  170.5 0.6 fusion
  171.1 0.6 slice.15
  (5 shorter events, 0.1 us)
Async XLA Ops:
  6.9 14.3 %all-to-all-start.1 = ((bf16[8,2,2560]{2,1,0:T(2,128)(2,1)}), bf16[8,2,2560]{2,1,0:T(2,128)(2,1)S(1)}, u32[]{:S(2)}, u32[]{:S(2)}) async-start(bf16[8,2,2560]{2,1,0:T(2,128)(2,1)} %reshape.73), calls=%async_computation.1 | async-start | bytes 163840 | tf_op jit(solution)/shard_map/all_to_all | solution.py:321
  22.3 62.5 %all-to-all-start = ((bf16[8,1,64,1024]{3,2,1,0:T(8,128)(2,1)}), bf16[8,1,64,1024]{3,2,1,0:T(8,128)(2,1)S(1)}, u32[]{:S(2)}, u32[]{:S(2)}) async-start(bf16[8,1,64,1024]{3,2,1,0:T(8,128)(2,1)} %broadcast_in_dim.48), calls=%async_computation | async-start | bytes 2097152 | tf_op jit(solution)/shard_map/all_to_all | solution.py:312
  84.8 1.0 copy-start
  106.1 26.6 %all-to-all-start.3 = ((bf16[8,64,1024]{2,1,0:T(8,128)(2,1)}), bf16[8,64,1024]{2,1,0:T(8,128)(2,1)S(1)}, u32[]{:S(2)}, u32[]{:S(2)}) async-start(bf16[8,64,1024]{2,1,0:T(8,128)(2,1)} %get-tuple-element.13), calls=%async_computation.3 | async-start | bytes 2097152 | tf_op jit(solution)/shard_map/all_to_all | solution.py:331
  111.2 58.6 %collective-permute-start = (f32[1,32,512]{2,1,0:T(8,128)S(1)}, f32[1,32,512]{2,1,0:T(8,128)S(1)}, u32[]{:S(2)}, u32[]{:S(2)}) collective-permute-start(f32[1,32,512]{2,1,0:T(8,128)S(1)} %all_to_all.40), channel_id=1, source_target_pairs={{0,8},{8,0},{1,9},{9,1},{2,10},{10,2},{3,11},{11,3},{4,12},{12,4},... | collective-permute-start | bytes 196616 | tf_op jit(solution)/shard_map/ppermute | solution.py:37
  132.8 37.6 %collective-permute-start.1 = (f32[1,64,1024]{2,1,0:T(8,128)S(1)}, f32[1,64,1024]{2,1,0:T(8,128)S(1)}, u32[]{:S(2)}, u32[]{:S(2)}) collective-permute-start(f32[1,64,1024]{2,1,0:T(8,128)S(1)} %bitcast.29), channel_id=1, source_target_pairs={{0,16},{16,0},{1,17},{17,1},{2,18},{18,2},{3,19},{19,3},{4,20},{20... | collective-permute-start | bytes 786440 | tf_op jit(solution)/shard_map/ppermute | solution.py:37

commit v2 on v1

v2 whole, which is shorter than its diff:
```python
import functools
import math

import jax
import jax.numpy as jnp
from jax import lax
from jax.experimental import pallas as pl
from jax.experimental.pallas import tpu as pltpu
from jax.sharding import PartitionSpec as P

F32 = jnp.float32
BF16 = jnp.bfloat16
RSQRT2 = 1.0 / math.sqrt(2.0)
EXP2_SCALE = -0.5 / math.log(2.0)
EXP2_SHIFT = math.log2(2.0 / math.sqrt(2.0 * math.pi))
ROWS = 16
LANES = 128
NT = (((1,), (1,)), ((), ()))
VMEM_LIMIT = 60 << 20


def full_spec(array):
    return pl.BlockSpec(array.shape, lambda *_: (0,) * array.ndim)


def divisor(total, largest):
    return math.gcd(total, largest)


def split_low(values, pieces):
    found = []
    for _ in range(pieces):
        piece = values.astype(BF16).astype(F32)
        found.append(piece)
        values = values - piece
    return found


def as_rows(pieces, count):
    rows = lax.broadcasted_iota(jnp.int32, (count, pieces[0].shape[1]), 0)
    block = jnp.zeros(rows.shape, F32)
    for place, piece in enumerate(pieces):
        block = jnp.where(rows == place, piece, block)
    return block.astype(BF16)


def eye(size):
    rows = lax.broadcasted_iota(jnp.int32, (size, size), 0)
    return jnp.where(rows == lax.broadcasted_iota(jnp.int32, (size, size), 1), 1.0, 0.0).astype(BF16)


def transposed(block):
    return lax.dot_general(eye(block.shape[1]), block, NT, preferred_element_type=F32)


def gain_columns(gain_row):
    chans = gain_row.shape[1]
    total = None
    for piece in split_low(gain_row, 3):
        spread = jnp.broadcast_to(piece, (LANES, chans)).astype(BF16)
        part = lax.dot_general(eye(chans), spread, NT, preferred_element_type=F32)
        total = part if total is None else total + part
    return total


def widen(block, tile):
    return jnp.concatenate([block] * (tile // block.shape[1]), axis=1)


def other_sum(values, name):
    if lax.axis_size(name) == 2:
        return lax.ppermute(values, name, [(0, 1), (1, 0)])
    return lax.psum(values, name) - values


def unit_norm(values):
    centre = values - jnp.mean(values, axis=0, keepdims=True)
    inv_std = lax.rsqrt(jnp.mean(centre * centre, axis=0, keepdims=True) + 1e-05)
    return centre * inv_std, inv_std


def pack_kernel(k_ref, v_ref, q_ref, dout_ref, out_ref, norm_ref, send_ref, *, rows):
    targets, own_heads, _, keys = send_ref.shape
    head_dim = k_ref.shape[1]
    begin = 2 * head_dim
    for head in range(own_heads):
        dout = dout_ref[head]
        deltas = jnp.sum(dout.astype(F32) * out_ref[head].astype(F32), axis=0, keepdims=True)
        scalars = split_low(norm_ref[head : head + 1, :], 3) + split_low(deltas, 3)
        packed = jnp.concatenate([q_ref[head], dout, as_rows(scalars, ROWS)], axis=0)
        for target in range(targets):
            send_ref[target, head, :head_dim, :] = k_ref[head]
            send_ref[target, head, head_dim:begin, :] = v_ref[head]
            slab = target * rows // LANES * LANES
            pieces = [
                packed[place : place + ROWS, slab : slab + LANES] for place in range(0, packed.shape[0], ROWS)
            ]
            fill = keys - LANES * len(pieces)
            if fill:
                pieces.append(jnp.zeros((ROWS, fill), BF16))
            send_ref[target, head, begin:, :] = jnp.concatenate(pieces, axis=1)


def pack_call(k_heads, v_heads, q_heads, dout_heads, out_heads, log_norm, targets, rows):
    own_heads, head_dim, keys = k_heads.shape
    return pl.pallas_call(
        functools.partial(pack_kernel, rows=rows),
        out_shape=jax.ShapeDtypeStruct((targets, own_heads, 2 * head_dim + ROWS, keys), BF16),
        compiler_params=pltpu.CompilerParams(vmem_limit_bytes=VMEM_LIMIT),
        name="pack_heads",
    )(k_heads, v_heads, q_heads, dout_heads, out_heads, log_norm)


def forward_kernel(
    pair_ref, bucket_ref, gain_ref, w_in_ref, b_in_ref, w_out_ref, table_ref, slope_ref, bias_ref, w_pre, w_mix,
    w_table, gain, *, group, tile
):
    rows, chans, keys = pair_ref.shape
    heads, buckets = w_table.shape
    key_tiles = keys // tile
    first_row = pl.program_id(0) * rows

    @pl.when(pl.program_id(0) == 0)
    def _():
        stacked = jnp.concatenate([w_in_ref[...], as_rows(split_low(b_in_ref[...], 3), ROWS)], axis=0)
        w_pre[...] = transposed(stacked).astype(BF16)
        w_mix[...] = (lax.dot_general(eye(heads), w_out_ref[...], NT, preferred_element_type=F32) * 0.5).astype(BF16)
        w_table[...] = lax.dot_general(eye(heads), table_ref[...], NT, preferred_element_type=F32).astype(BF16)
        gain[...] = gain_columns(gain_ref[...])

    ones = jnp.where(lax.broadcasted_iota(jnp.int32, (ROWS, tile), 0) < 3, 1.0, 0.0).astype(BF16)

    def one_row(row, cols):
        unit_pairs, _ = unit_norm(pair_ref[row, :, cols].astype(F32))
        normed = (unit_pairs * widen(gain[...], tile)).astype(BF16)
        pre_act = jnp.dot(w_pre[...], jnp.concatenate([normed, ones], axis=0), preferred_element_type=F32)
        cdf2 = lax.erf(pre_act * RSQRT2) + 1.0
        hidden2 = (pre_act * cdf2).astype(BF16)
        density2 = jnp.exp2(pre_act * pre_act * EXP2_SCALE + EXP2_SHIFT)
        slope_ref[row, :, cols] = (cdf2 + pre_act * density2).astype(BF16)
        bucket_iota = lax.broadcasted_iota(jnp.int32, (buckets, tile), 0)
        onehot = jnp.where(bucket_ref[pl.ds(first_row + row, 1), cols] == bucket_iota, 1.0, 0.0).astype(BF16)
        mixed = jnp.dot(w_mix[...], hidden2, preferred_element_type=F32)
        return mixed + jnp.dot(w_table[...], onehot, preferred_element_type=F32)

    def step(index, carry):
        row_group = index // key_tiles
        cols = pl.ds(pl.multiple_of((index % key_tiles) * tile, tile), tile)
        outs = [one_row(row_group * group + member, cols) for member in range(group)]
        size = group * heads
        bias_ref[pl.ds(pl.multiple_of(row_group * size, size), size), cols] = jnp.concatenate(
            outs, axis=0
        ).astype(BF16)
        return carry

    lax.fori_loop(0, (rows // group) * key_tiles, step, 0)


def forward_call(pair_feats, bucket_ids, gain, w_in, b_in, w_out, table):
    rows, chans, keys = pair_feats.shape
    hid, heads = w_out.shape
    block = divisor(rows, 4)
    return pl.pallas_call(
        functools.partial(forward_kernel, group=block, tile=divisor(keys, 512)),
        grid=(rows // block,),
        in_specs=[
            pl.BlockSpec((block, chans, keys), lambda i: (i, 0, 0)),
            full_spec(bucket_ids),
            full_spec(gain),
            full_spec(w_in),
            full_spec(b_in),
            full_spec(w_out),
            full_spec(table),
        ],
        out_specs=[
            pl.BlockSpec((block, hid, keys), lambda i: (i, 0, 0)),
            pl.BlockSpec((block * heads, keys), lambda i: (i, 0)),
        ],
        out_shape=[
            jax.ShapeDtypeStruct((rows, hid, keys), BF16),
            jax.ShapeDtypeStruct((rows * heads, keys), BF16),
        ],
        scratch_shapes=[
            pltpu.VMEM((hid, chans + ROWS), BF16),
            pltpu.VMEM((heads, hid), BF16),
            pltpu.VMEM((heads, table.shape[0]), BF16),
            pltpu.VMEM((chans, LANES), F32),
        ],
        compiler_params=pltpu.CompilerParams(vmem_limit_bytes=VMEM_LIMIT),
        cost_estimate=pl.CostEstimate(
            flops=2 * rows * keys * hid * 256,
            bytes_accessed=2 * rows * keys * (hid + chans),
            transcendentals=2 * rows * keys * hid,
        ),
        name="pair_forward",
    )(pair_feats, bucket_ids, gain, w_in, b_in, w_out, table)


def attention_kernel(
    bias_ref, kv_ref, aux_ref, mask_ref, ds_ref, part_ref, q_rows, d_rows, q_cols, d_cols, norm_ref, delta_ref,
    dq_acc, *, head_dim, rows
):
    heads = kv_ref.shape[0]
    tile = bias_ref.shape[1]
    width = heads * head_dim
    flat = rows * heads
    scale = 1.0 / math.sqrt(head_dim)
    step = pl.program_id(0)
    cols = pl.ds(pl.multiple_of(step * tile, tile), tile)
    offset = lax.rem(lax.axis_index("heads") * rows, LANES)
    groups = head_dim // ROWS

    def spread_matrix():
        lane = lax.broadcasted_iota(jnp.int32, (flat, LANES), 1)
        return lane == lax.broadcasted_iota(jnp.int32, (flat, LANES), 0) // heads + offset

    def own_columns():
        return (
            lax.broadcasted_iota(jnp.int32, (width, flat), 1) % heads
            == lax.broadcasted_iota(jnp.int32, (width, flat), 0) // head_dim
        )

    @pl.when(step == 0)
    def _():
        spread_low = jnp.where(spread_matrix(), 1.0, 0.0).astype(BF16)
        own_rows = (
            lax.broadcasted_iota(jnp.int32, (flat, width), 0) % heads
            == lax.broadcasted_iota(jnp.int32, (flat, width), 1) // head_dim
        )
        own_cols = own_columns()
        for begin, by_rows, by_cols in ((0, q_rows, q_cols), (groups, d_rows, d_cols)):
            block = jnp.concatenate(
                [aux_ref[:, :, (begin + part) * LANES : (begin + part + 1) * LANES] for part in range(groups)], axis=1
            ).reshape(width, LANES)
            spread = lax.dot_general(spread_low, block, NT, preferred_element_type=F32)
            by_rows[...] = jnp.where(own_rows, spread, 0.0).astype(BF16)
            spread = lax.dot_general(block, spread_low, NT, preferred_element_type=F32)
            by_cols[...] = jnp.where(own_cols, spread, 0.0).astype(BF16)
        tail = aux_ref[:, :, 2 * groups * LANES : (2 * groups + 1) * LANES].astype(F32)
        lane = lax.broadcasted_iota(jnp.int32, (rows, heads, LANES), 2)
        own_lane = lane == lax.broadcasted_iota(jnp.int32, (rows, heads, LANES), 0) + offset
        for begin, target in ((0, norm_ref), (3, delta_ref)):
            pieces = tail[:, begin, :] + tail[:, begin + 1, :] + tail[:, begin + 2, :]
            column = jnp.sum(jnp.where(own_lane, pieces[None], 0.0), axis=2, keepdims=True)
            target[...] = jnp.broadcast_to(column.reshape(flat, 1), target.shape)
        dq_acc[...] = jnp.zeros_like(dq_acc)

    norm = widen(norm_ref[...], tile)
    delta = widen(delta_ref[...], tile)
    keys = kv_ref[:, :head_dim, :].reshape(width, tile)
    values = kv_ref[:, head_dim:, :].reshape(width, tile)
    scores = jnp.dot(q_rows[...], keys, preferred_element_type=F32) * scale + bias_ref[...].astype(F32)
    probs = jnp.where(mask_ref[...] == 1, jnp.exp(scores - norm), 0.0)
    dprobs = jnp.dot(d_rows[...], values, preferred_element_type=F32)
    dscores = (probs * (dprobs - delta)).astype(BF16)
    ds_ref[...] = dscores
    dk_part = jnp.dot(q_cols[...], dscores, preferred_element_type=F32)
    dv_part = jnp.dot(d_cols[...], probs.astype(BF16), preferred_element_type=F32)
    part_ref[:, :head_dim, cols] = dk_part.reshape(heads, head_dim, tile).astype(BF16)
    part_ref[:, head_dim : 2 * head_dim, cols] = dv_part.reshape(heads, head_dim, tile).astype(BF16)
    dq_acc[...] += lax.dot_general(keys, dscores, NT, preferred_element_type=F32)

    @pl.when(step == pl.num_programs(0) - 1)
    def _():
        spread_low = jnp.where(spread_matrix(), 1.0, 0.0).astype(BF16)
        total = None
        for piece in split_low(jnp.where(own_columns(), dq_acc[...], 0.0), 3):
            part = jnp.dot(piece.astype(BF16), spread_low, preferred_element_type=F32)
            total = part if total is None else total + part
        pieces = []
        for piece in split_low(total, 2):
            block = piece.astype(BF16).reshape(heads, head_dim, LANES)
            pieces += [block[:, place : place + ROWS, :] for place in range(0, head_dim, ROWS)]
        fill = part_ref.shape[2] - LANES * len(pieces)
        if fill:
            pieces.append(jnp.zeros((heads, ROWS, fill), BF16))
        part_ref[:, 2 * head_dim :, :] = jnp.concatenate(pieces, axis=2)


def attention_call(bias, received, key_mask, head_dim, rows):
    flat, keys = bias.shape
    heads, depth, _ = received.shape
    width = heads * head_dim
    tile = divisor(keys, 256)
    return pl.pallas_call(
        functools.partial(attention_kernel, head_dim=head_dim, rows=rows),
        grid=(keys // tile,),
        in_specs=[
            pl.BlockSpec((flat, tile), lambda i: (0, i)),
            pl.BlockSpec((heads, 2 * head_dim, tile), lambda i: (0, 0, i)),
            pl.BlockSpec((heads, ROWS, keys), lambda i: (0, 2 * head_dim // ROWS, 0)),
            pl.BlockSpec((1, tile), lambda i: (0, i)),
        ],
        out_specs=[
            pl.BlockSpec((flat, tile), lambda i: (0, i)),
            pl.BlockSpec((heads, depth, keys), lambda i: (0, 0, 0)),
        ],
        out_shape=[
            jax.ShapeDtypeStruct((flat, keys), BF16),
            jax.ShapeDtypeStruct((heads, depth, keys), BF16),
        ],
        scratch_shapes=[
            pltpu.VMEM((flat, width), BF16),
            pltpu.VMEM((flat, width), BF16),
            pltpu.VMEM((width, flat), BF16),
            pltpu.VMEM((width, flat), BF16),
            pltpu.VMEM((flat, LANES), F32),
            pltpu.VMEM((flat, LANES), F32),
            pltpu.VMEM((width, flat), F32),
        ],
        compiler_params=pltpu.CompilerParams(vmem_limit_bytes=VMEM_LIMIT),
        cost_estimate=pl.CostEstimate(
            flops=10 * flat * keys * width, bytes_accessed=8 * flat * keys, transcendentals=flat * keys
        ),
        name="pair_attention",
    )(bias, received, received, key_mask.reshape(1, keys))


def backward_kernel(
    pair_ref, ds_ref, slope_ref, gain_ref, w_in_ref, w_out_ref, *rest, group, tile
):
    out_ref, w_back, gain = rest[-3:]
    rows, chans, keys = pair_ref.shape
    heads = w_back.shape[1]
    key_tiles = keys // tile

    @pl.when(pl.program_id(0) == 0)
    def _():
        w_back[...] = (w_out_ref[...].astype(F32) * 0.5).astype(BF16)
        gain[...] = gain_columns(gain_ref[...])

    def step(index, carry):
        row_group = index // key_tiles
        cols = pl.ds(pl.multiple_of((index % key_tiles) * tile, tile), tile)
        size = group * heads
        dscores = ds_ref[pl.ds(pl.multiple_of(row_group * size, size), size), cols]
        for member in range(group):
            row = row_group * group + member
            unit_pairs, inv_std = unit_norm(pair_ref[row, :, cols].astype(F32))
            dhidden = jnp.dot(
                w_back[...], dscores[member * heads : (member + 1) * heads], preferred_element_type=F32
            )
            dpre = dhidden.astype(BF16) * slope_ref[row, :, cols]
            dunit = jnp.dot(w_in_ref[...], dpre, preferred_element_type=F32) * widen(gain[...], tile)
            first_mean = jnp.mean(dunit, axis=0, keepdims=True)
            second_mean = jnp.mean(dunit * unit_pairs, axis=0, keepdims=True)
            grad = inv_std * (dunit - first_mean - unit_pairs * second_mean)
            out_ref[row, :, cols] = grad.astype(BF16)
        return carry

    lax.fori_loop(0, (rows // group) * key_tiles, step, 0)


def backward_call(pair_feats, dscores, slope, gain, w_in, w_out, begin, count, previous):
    rows, chans, keys = pair_feats.shape
    hid, heads = w_out.shape
    block = divisor(math.gcd(begin, count), 4)
    first = begin // block
    operands = [pair_feats, dscores, slope, gain, w_in, w_out]
    in_specs = [
        pl.BlockSpec((block, chans, keys), lambda i: (i + first, 0, 0)),
        pl.BlockSpec((block * heads, keys), lambda i: (i + first, 0)),
        pl.BlockSpec((block, hid, keys), lambda i: (i + first, 0, 0)),
        full_spec(gain),
        full_spec(w_in),
        full_spec(w_out),
    ]
    aliases = {}
    if previous is not None:
        aliases = {len(operands): 0}
        operands.append(previous)
        in_specs.append(pl.BlockSpec(memory_space=pl.ANY))
    return pl.pallas_call(
        functools.partial(backward_kernel, group=block, tile=divisor(keys, 512)),
        grid=(count // block,),
        in_specs=in_specs,
        out_specs=pl.BlockSpec((block, chans, keys), lambda i: (i + first, 0, 0)),
        out_shape=jax.ShapeDtypeStruct((rows, chans, keys), BF16),
        scratch_shapes=[pltpu.VMEM((hid, heads), BF16), pltpu.VMEM((chans, LANES), F32)],
        input_output_aliases=aliases,
        compiler_params=pltpu.CompilerParams(vmem_limit_bytes=VMEM_LIMIT),
        cost_estimate=pl.CostEstimate(
            flops=2 * count * keys * hid * 256,
            bytes_accessed=2 * count * keys * (hid + 2 * chans),
            transcendentals=0,
        ),
        name="pair_backward",
    )(*operands)


def sum_kernel(part_ref, dkv_ref, dq_ref, *, head_dim, rows):
    sources, own_heads, _, keys = part_ref.shape
    for head in range(own_heads):
        total = part_ref[0, head, : 2 * head_dim, :].astype(F32)
        for source in range(1, sources):
            total = total + part_ref[source, head, : 2 * head_dim, :].astype(F32)
        dkv_ref[head] = total
        dq_ref[head] = jnp.zeros(dq_ref.shape[1:], F32)
        for source in range(sources):
            slab = source * rows // LANES * LANES
            groups = head_dim // ROWS
            for part in range(2 * groups):
                piece = part_ref[source, head, 2 * head_dim :, part * LANES : (part + 1) * LANES].astype(F32)
                place = part % groups * ROWS
                dq_ref[head, place : place + ROWS, slab : slab + LANES] += piece


def sum_call(parts, head_dim, rows, queries):
    _, own_heads, _, keys = parts.shape
    return pl.pallas_call(
        functools.partial(sum_kernel, head_dim=head_dim, rows=rows),
        out_shape=[
            jax.ShapeDtypeStruct((own_heads, 2 * head_dim, keys), F32),
            jax.ShapeDtypeStruct((own_heads, head_dim, queries), F32),
        ],
        compiler_params=pltpu.CompilerParams(vmem_limit_bytes=VMEM_LIMIT),
        name="sum_sources",
    )(parts)


def finish_kernel(dkv_ref, dkv_other, dq_ref, dq_other, grad_q, grad_k, grad_v, *, head_dim):
    scale = 1.0 / math.sqrt(head_dim)
    total = dkv_ref[...] + dkv_other[...]
    grad_q[...] = ((dq_ref[...] + dq_other[...]) * scale).astype(BF16)
    grad_k[...] = (total[:, :head_dim, :] * scale).astype(BF16)
    grad_v[...] = total[:, head_dim:, :].astype(BF16)


def finish_call(dkv, dkv_other, dq, dq_other):
    own_heads, head_dim, queries = dq.shape
    keys = dkv.shape[2]
    return pl.pallas_call(
        functools.partial(finish_kernel, head_dim=head_dim),
        out_shape=[
            jax.ShapeDtypeStruct((own_heads, head_dim, queries), BF16),
            jax.ShapeDtypeStruct((own_heads, head_dim, keys), BF16),
            jax.ShapeDtypeStruct((own_heads, head_dim, keys), BF16),
        ],
        compiler_params=pltpu.CompilerParams(vmem_limit_bytes=VMEM_LIMIT),
        name="finish",
    )(dkv, dkv_other, dq, dq_other)


def per_device(
    pair_feats,
    bucket_ids,
    ln_gain,
    w_in,
    b_in,
    w_out,
    bucket_table,
    key_mask,
    q_heads,
    k_heads,
    v_heads,
    out_heads,
    dout_heads,
    log_norm,
):
    axis_size = lax.axis_size("heads")
    own_heads, head_dim, queries = q_heads.shape
    rows = pair_feats.shape[0]
    gain = ln_gain.reshape(1, -1)

    packed = pack_call(k_heads, v_heads, q_heads, dout_heads, out_heads, log_norm, axis_size, rows)
    received = lax.all_to_all(packed, "heads", split_axis=0, concat_axis=0, tiled=True)
    slope, bias_vals = forward_call(
        pair_feats, bucket_ids, gain, w_in, b_in.reshape(1, -1), w_out, bucket_table
    )
    received = received.reshape((axis_size * own_heads,) + received.shape[2:])
    dscores, parts = attention_call(bias_vals, received, key_mask, head_dim, rows)
    parts = lax.all_to_all(
        parts.reshape((axis_size, own_heads) + parts.shape[1:]), "heads", split_axis=0, concat_axis=0, tiled=True
    )
    last = rows // 4
    weights = (gain, w_in, w_out)
    grad_pairs = backward_call(pair_feats, dscores, slope, *weights, 0, rows - last, None)
    parts, grad_pairs = lax.optimization_barrier((parts, grad_pairs))
    dkv_sum, dq_sum = sum_call(parts, head_dim, rows, queries)
    grad_pairs, dkv_sum, dq_sum = lax.optimization_barrier((grad_pairs, dkv_sum, dq_sum))
    dkv_other = other_sum(dkv_sum, "query")
    dq_other = other_sum(dq_sum, "key")
    grad_pairs = backward_call(pair_feats, dscores, slope, *weights, rows - last, last, grad_pairs)
    grad_q, grad_k, grad_v = finish_call(dkv_sum, dkv_other, dq_sum, dq_other)
    return (grad_pairs, grad_q, grad_k, grad_v)


def solution(mesh):
    def traced(*args):
        with jax.sharding.use_abstract_mesh(mesh.abstract_mesh):
            return jax.shard_map(
                per_device,
                mesh=mesh,
                in_specs=(
                    P(("query", "heads"), None, "key"),
                    P(("query", "heads"), "key"),
                    P(),
                    P(),
                    P(),
                    P(),
                    P(),
                    P("key"),
                    P("heads", None, "query"),
                    P("heads", None, "key"),
                    P("heads", None, "key"),
                    P("heads", None, "query"),
                    P("heads", None, "query"),
                    P("heads", "query"),
                ),
                out_specs=(
                    P(("query", "heads"), None, "key"),
                    P("heads", None, "query"),
                    P("heads", None, "key"),
                    P("heads", None, "key"),
                ),
                check_vma=False,
            )(*args)

    return traced
```

time: 173 us -> 131 us (0.76)
  waiting for transfers between devices: 26 us -> 2.89 us
  Pallas kernels: 93.3 us -> 106 us
  blocking collectives: 12.6 us -> 0 us
  local copies, waits for them, and re-layouts: 15.5 us -> 6.18 us
  other arithmetic: 7.42 us -> 0 us
    all_to_all x3 -> x2, waiting for transfers between devices: 26 us -> 2.88 us  [the longest x1 2.88 us: per_device(): lax.all_to_all(parts.reshape((axis_size, own_heads) + parts.shape[1:]), '...]
    pallas_call x3 -> x7, Pallas kernels: 93.3 us -> 106 us  [the longest x1 54.6 us: forward_call(): pl.pallas_call(functools.partial(forward_kernel, group=block, tile=diviso...]
    all_to_all x1 -> x0, blocking collectives: 12.6 us -> none  [per_device(): lax.all_to_all(dq_part, 'heads', split_axis=0, concat_axis=2, tiled=True)]
    broadcast_in_dim x8 -> x0, local copies, waits for them, and re-layouts: 4.6 us -> none  [the longest x1 1.84 us: forward_call(): bucket_ids[:, None, :]]
    concatenate x3 -> x0, local copies, waits for them, and re-layouts: 2.65 us -> none  [the longest x2 1.85 us: per_device(): jnp.concatenate([q_heads, dout_heads] + scalars + [jnp.zeros((own_heads,...]
    convert_element_type x4 -> x0, other arithmetic: 1.97 us -> none  [the longest x2 0.7 us: split_three(): return [piece.astype(BF16) for piece in (high, mid, low)]]
    all_to_all x3 -> x2, starting transfers between devices: 14.4 us -> 13.3 us  [the longest x1 7.31 us: per_device(): lax.all_to_all(packed, 'heads', split_axis=0, concat_axis=0, tiled=True)]
  transfers between devices with their start and end apart: 5 -> 4, of which waited for: 2 -> 1; matrix products, arithmetic and copies ran while one was open for 7% -> 2% of each run, Pallas kernels for 51% -> 72%
where the time goes in v2:
time: 131 us
  Pallas kernels  106 us (81%)
  starting transfers between devices  14.8 us (11%)
  local copies, waits for them, and re-layouts  6.18 us (5%)
  waiting for transfers between devices  2.89 us (2%)
    pallas_call x1, Pallas kernels, forward_call(): pl.pallas_call(functools.partial(forward_kernel, group=block, tile=diviso...  54.6 us
    pallas_call x2, Pallas kernels, backward_call(): pl.pallas_call(functools.partial(backward_kernel, group=block, tile=divis...  39.2 us
    all_to_all x1, starting transfers between devices, per_device(): lax.all_to_all(packed, 'heads', split_axis=0, concat_axis=0, tiled=True)  7.31 us
    pallas_call x1, Pallas kernels, attention_call(): pl.pallas_call(functools.partial(attention_kernel, head_dim=head_dim, row...  6.42 us
    unnamed x10, local copies, waits for them, and re-layouts  6.18 us
    all_to_all x1, starting transfers between devices, per_device(): lax.all_to_all(parts.reshape((axis_size, own_heads) + parts.shape[1:]), '...  6 us
    all_to_all x1, waiting for transfers between devices, per_device(): lax.all_to_all(parts.reshape((axis_size, own_heads) + parts.shape[1:]), '...  2.88 us
  transfers between devices with their start and end apart: 4, of which 1 were waited for; matrix products, arithmetic and copies ran while one was open for 2% of the time, Pallas kernels for 72%

profile of v2, /device:TPU:0, one launch (start us, length us, event | category | flops | bytes accessed | tf_op | source)
XLA Modules:
  0.0 130.7 jit_solution(4036607864616267361)
XLA Ops:
  0.6 2.0 %pack_heads.1 = bf16[8,1,80,1024]{3,2,1,0:T(8,128)(2,1)} custom-call(bf16[1,32,1024]{2,1,0:T(8,128)(2,1)} %k_ref.1, bf16[1,32,1024]{2,1,0:T(8,128)(2,1)} %v_ref.1, bf16[1,32,512]{2,1,0:T(8,128)(2,1)} %q_ref.1, bf16[1,32,512]{2,1,0:T(8,128)(2,1)} %dout_ref.1, bf16[1,32,512]{2,1,0:T(8,128)(2,1)} %out_ref.1, f32[1,512]{1,0:T(1,128)} %norm_ref.1), custom_call_target="tpu_custom_call" | custom-call | tf_op jit(solution)/shard_map/pack_heads/pallas_call | solution.py:106
  2.7 7.3 %all-to-all-start = ((bf16[8,1,80,1024]{3,2,1,0:T(8,128)(2,1)}), bf16[8,1,80,1024]{3,2,1,0:T(8,128)(2,1)S(1)}, u32[]{:S(2)}, u32[]{:S(2)}) async-start(bf16[8,1,80,1024]{3,2,1,0:T(8,128)(2,1)} %pack_heads.1), calls=%async_computation | async-start | bytes 2621440 | tf_op jit(solution)/shard_map/all_to_all | solution.py:466
  10.0 1.4 %copy.24.w_out_ref = bf16[256,8]{1,0:T(8,128)(2,1)} copy(bf16[256,8]{0,1:T(8,128)(2,1)} %param.19) | data formatting | bytes 8192 | tf_op args[5]
  11.4 1.4 %copy.25.table_ref = bf16[32,8]{1,0:T(8,128)(2,1)} copy(bf16[32,8]{0,1:T(8,128)(2,1)} %param.20) | data formatting | bytes 1024 | tf_op args[6]
  12.8 54.6 %pair_forward.1 = (bf16[64,256,1024]{2,1,0:T(8,128)(2,1)}, bf16[512,1024]{1,0:T(8,128)(2,1)}) custom-call(bf16[64,64,1024]{2,1,0:T(8,128)(2,1)} %pair_ref.5, s32[64,1024]{1,0:T(8,128)} %bucket_ref.1, f32[1,64]{1,0:T(1,128)} %bitcast.8, bf16[64,256]{1,0:T(8,128)(2,1)} %w_in_ref.5, f32[1,256]{1,0:T(1,128)} %bitcast.12, bf16[256,8]{1,0:T(8,128)(2,1)} %copy.24.w_out_ref, ...), custom_call_target="tpu_custom_call" | custom-call | flops 8589934592 | bytes 41943040 | tf_op jit(solution)/shard_map/pair_forward/pallas_call | solution.py:163
  67.4 0.0 all-to-all-done
  67.4 0.0 copy-start.1
  67.4 1.0 copy-done.1
  68.5 6.4 %pair_attention.1 = (bf16[512,1024]{1,0:T(8,128)(2,1)}, bf16[8,80,1024]{2,1,0:T(8,128)(2,1)}) custom-call(bf16[512,1024]{1,0:T(8,128)(2,1)} %get-tuple-element.18.bias_ref, bf16[8,80,1024]{2,1,0:T(8,128)(2,1)} %bitcast.5, bf16[8,80,1024]{2,1,0:T(8,128)(2,1)} %bitcast.6, s32[1,1024]{1,0:T(1,128)} %bitcast.11), custom_call_target="tpu_custom_call" | custom-call | flops 1342177280 | bytes 4194304 | tf_op jit(solution)/shard_map/pair_attention/pallas_call | solution.py:285
  74.9 6.0 %all-to-all-start.1 = ((bf16[8,1,80,1024]{3,2,1,0:T(8,128)(2,1)}), bf16[8,1,80,1024]{3,2,1,0:T(8,128)(2,1)S(1)}, u32[]{:S(2)}, u32[]{:S(2)}) async-start(bf16[8,1,80,1024]{3,2,1,0:T(8,128)(2,1)} %bitcast.7), calls=%async_computation.1 | async-start | bytes 2621440 | tf_op jit(solution)/shard_map/all_to_all | solution.py:472
  80.9 28.0 %pair_backward.2.rest_0_ = bf16[64,64,1024]{2,1,0:T(8,128)(2,1)} custom-call(bf16[64,64,1024]{2,1,0:T(8,128)(2,1)} %pair_ref.5, bf16[512,1024]{1,0:T(8,128)(2,1)} %get-tuple-element.19.ds_ref, bf16[64,256,1024]{2,1,0:T(8,128)(2,1)} %get-tuple-element.20.slope_ref, f32[1,64]{1,0:T(1,128)} %bitcast.9, bf16[64,256]{1,0:T(8,128)(2,1)} %w_in_ref.5, ...), custom_call_target="tpu_custom_call" | custom-call | flops 6442450944 | bytes 37748736 | tf_op jit(solution)/shard_map/pair_backward/pallas_call | solution.py:373
  108.9 2.9 %all-to-all-done.1.part_ref = bf16[8,1,80,1024]{3,2,1,0:T(8,128)(2,1)S(1)} async-done(((bf16[8,1,80,1024]{3,2,1,0:T(8,128)(2,1)}), bf16[8,1,80,1024]{3,2,1,0:T(8,128)(2,1)S(1)}, u32[]{:S(2)}, u32[]{:S(2)}) %all-to-all-start.1) | async-done | bytes 1310752 | tf_op jit(solution)/shard_map/all_to_all | solution.py:472
  111.8 0.0 copy-start
  111.8 1.1 copy-done
  112.8 2.2 %sum_sources.1 = (f32[1,64,1024]{2,1,0:T(8,128)}, f32[1,32,512]{2,1,0:T(8,128)}) custom-call(bf16[8,1,80,1024]{3,2,1,0:T(8,128)(2,1)} %copy-done), custom_call_target="tpu_custom_call" | custom-call | tf_op jit(solution)/shard_map/sum_sources/pallas_call | solution.py:410
  115.1 0.0 collective-permute-start
  115.1 1.5 %collective-permute-start.1 = (f32[1,32,512]{2,1,0:T(8,128)}, f32[1,32,512]{2,1,0:T(8,128)S(1)}, u32[]{:S(2)}, u32[]{:S(2)}) collective-permute-start(f32[1,32,512]{2,1,0:T(8,128)} %get-tuple-element.28.dq_ref), channel_id=1, source_target_pairs={{0,8},{8,0},{1,9},{9,1},{2,10},{10,2},{3,11},{11,3},{4,12},{12,4},... | collective-permute-start | bytes 196616 | tf_op jit(solution)/shard_map/ppermute | solution.py:72
  116.6 11.1 %pair_backward.3 = bf16[64,64,1024]{2,1,0:T(8,128)(2,1)} custom-call(bf16[64,64,1024]{2,1,0:T(8,128)(2,1)} %pair_ref.5, bf16[512,1024]{1,0:T(8,128)(2,1)} %get-tuple-element.19.ds_ref, bf16[64,256,1024]{2,1,0:T(8,128)(2,1)} %get-tuple-element.20.slope_ref, f32[1,64]{1,0:T(1,128)} %bitcast.10, ...), custom_call_target="tpu_custom_call", output_to_operand_aliasing={{}: (6, {})} | custom-call | flops 2147483648 | bytes 12582912 | tf_op jit(solution)/shard_map/pair_backward/pallas_call | solution.py:373
  127.7 0.0 collective-permute-done.1.dq_other
  127.7 0.0 copy-start.3
  127.7 0.0 collective-permute-done.dkv_other
  127.7 0.6 copy-done.3
  128.3 0.0 copy-start.2
  128.3 0.7 copy-done.2
  129.0 1.7 %finish.1 = (bf16[1,32,512]{2,1,0:T(8,128)(2,1)}, bf16[1,32,1024]{2,1,0:T(8,128)(2,1)}, bf16[1,32,1024]{2,1,0:T(8,128)(2,1)}) custom-call(f32[1,64,1024]{2,1,0:T(8,128)} %get-tuple-element.27.dkv_ref, f32[1,64,1024]{2,1,0:T(8,128)} %copy-done.2, f32[1,32,512]{2,1,0:T(8,128)} %get-tuple-element.28.dq_ref, f32[1,32,512]{2,1,0:T(8,128)} %copy-done.3), custom_call_target="tpu_custom_call" | custom-call | tf_op jit(solution)/shard_map/finish/pallas_call | solution.py:432
Async XLA Ops:
  2.7 64.7 %all-to-all-start = ((bf16[8,1,80,1024]{3,2,1,0:T(8,128)(2,1)}), bf16[8,1,80,1024]{3,2,1,0:T(8,128)(2,1)S(1)}, u32[]{:S(2)}, u32[]{:S(2)}) async-start(bf16[8,1,80,1024]{3,2,1,0:T(8,128)(2,1)} %pack_heads.1), calls=%async_computation | async-start | bytes 2621440 | tf_op jit(solution)/shard_map/all_to_all | solution.py:466
  67.4 1.1 copy-start.1
  74.9 36.9 %all-to-all-start.1 = ((bf16[8,1,80,1024]{3,2,1,0:T(8,128)(2,1)}), bf16[8,1,80,1024]{3,2,1,0:T(8,128)(2,1)S(1)}, u32[]{:S(2)}, u32[]{:S(2)}) async-start(bf16[8,1,80,1024]{3,2,1,0:T(8,128)(2,1)} %bitcast.7), calls=%async_computation.1 | async-start | bytes 2621440 | tf_op jit(solution)/shard_map/all_to_all | solution.py:472
  111.8 1.1 copy-start
  115.1 12.7 %collective-permute-start = (f32[1,64,1024]{2,1,0:T(8,128)}, f32[1,64,1024]{2,1,0:T(8,128)S(1)}, u32[]{:S(2)}, u32[]{:S(2)}) collective-permute-start(f32[1,64,1024]{2,1,0:T(8,128)} %get-tuple-element.27.dkv_ref), channel_id=1, source_target_pairs={{0,16},{16,0},{1,17},{17,1},{2,18},{18,2},{3,19},{19,3},{4,20},{20... | collective-permute-start | bytes 786440 | tf_op jit(solution)/shard_map/ppermute | solution.py:72
  115.1 12.6 %collective-permute-start.1 = (f32[1,32,512]{2,1,0:T(8,128)}, f32[1,32,512]{2,1,0:T(8,128)S(1)}, u32[]{:S(2)}, u32[]{:S(2)}) collective-permute-start(f32[1,32,512]{2,1,0:T(8,128)} %get-tuple-element.28.dq_ref), channel_id=1, source_target_pairs={{0,8},{8,0},{1,9},{9,1},{2,10},{10,2},{3,11},{11,3},{4,12},{12,4},... | collective-permute-start | bytes 196616 | tf_op jit(solution)/shard_map/ppermute | solution.py:72
  127.7 0.6 copy-start.3
  128.3 0.7 copy-start.2

commit v3 on v2

v3 whole, which is shorter than its diff:
```python
import functools
import math

import jax
import jax.numpy as jnp
from jax import lax
from jax.experimental import pallas as pl
from jax.experimental.pallas import tpu as pltpu
from jax.sharding import PartitionSpec as P

F32 = jnp.float32
BF16 = jnp.bfloat16
RSQRT2 = 1.0 / math.sqrt(2.0)
EXP2_SCALE = -0.5 / math.log(2.0)
EXP2_SHIFT = math.log2(2.0 / math.sqrt(2.0 * math.pi))
ROWS = 16
LANES = 128
NT = (((1,), (1,)), ((), ()))
FULL_LIMIT = 60 << 20
BIG_LIMIT = 32 << 20
SMALL_LIMIT = 16 << 20


def low(value):
    return jnp.asarray(value, BF16)


def full_spec(array):
    return pl.BlockSpec(array.shape, lambda *_: (0,) * array.ndim)


def divisor(total, largest):
    return math.gcd(total, largest)


def split_low(values, pieces):
    found = []
    for _ in range(pieces):
        piece = values.astype(BF16).astype(F32)
        found.append(piece)
        values = values - piece
    return found


def as_rows(pieces, count):
    rows = lax.broadcasted_iota(jnp.int32, (count, pieces[0].shape[1]), 0)
    block = jnp.zeros(rows.shape, F32)
    for place, piece in enumerate(pieces):
        block = jnp.where(rows == place, piece, block)
    return block.astype(BF16)


def eye(size):
    rows = lax.broadcasted_iota(jnp.int32, (size, size), 0)
    return jnp.where(rows == lax.broadcasted_iota(jnp.int32, (size, size), 1), 1.0, 0.0).astype(BF16)


def transposed(block):
    return lax.dot_general(eye(block.shape[1]), block, NT, preferred_element_type=F32)


def gain_columns(gain_row):
    chans = gain_row.shape[1]
    total = None
    for piece in split_low(gain_row, 3):
        spread = jnp.broadcast_to(piece, (LANES, chans)).astype(BF16)
        part = lax.dot_general(eye(chans), spread, NT, preferred_element_type=F32)
        total = part if total is None else total + part
    return total


def widen(block, tile):
    return jnp.concatenate([block] * (tile // block.shape[1]), axis=1)


def other_sum(values, name):
    if lax.axis_size(name) == 2:
        return lax.ppermute(values, name, [(0, 1), (1, 0)])
    return lax.psum(values, name) - values


def pack_kernel(k_ref, v_ref, q_ref, dout_ref, out_ref, norm_ref, send_ref, *, rows):
    targets, own_heads, depth, lanes = send_ref.shape
    head_dim = k_ref.shape[1]
    keys = lanes - LANES
    half = LANES // 2
    lane = lax.broadcasted_iota(jnp.int32, (depth, LANES), 1)
    for head in range(own_heads):
        dout = dout_ref[head]
        deltas = jnp.sum(dout.astype(F32) * out_ref[head].astype(F32), axis=0, keepdims=True)
        scalars = as_rows(split_low(norm_ref[head : head + 1, :], 3) + split_low(deltas, 3), depth).astype(F32)
        heads_part = jnp.concatenate([q_ref[head], dout], axis=0).astype(F32)
        for target in range(targets):
            send_ref[target, head, :head_dim, :keys] = k_ref[head]
            send_ref[target, head, head_dim:, :keys] = v_ref[head]
            slab = target * rows // LANES * LANES
            window = (lane >= target * rows - slab) & (lane < target * rows - slab + rows)
            turned = [scalars[:, slab + half : slab + LANES], scalars[:, slab : slab + half]]
            extra = jnp.where(window, heads_part[:, slab : slab + LANES], jnp.concatenate(turned, axis=1))
            send_ref[target, head, :, keys:] = extra.astype(BF16)


def pack_call(k_heads, v_heads, q_heads, dout_heads, out_heads, log_norm, targets, rows):
    own_heads, head_dim, keys = k_heads.shape
    return pl.pallas_call(
        functools.partial(pack_kernel, rows=rows),
        out_shape=jax.ShapeDtypeStruct((targets, own_heads, 2 * head_dim, keys + LANES), BF16),
        compiler_params=pltpu.CompilerParams(vmem_limit_bytes=FULL_LIMIT),
        name="pack_heads",
    )(k_heads, v_heads, q_heads, dout_heads, out_heads, log_norm)


def unit_norm(values):
    centre = values - jnp.mean(values, axis=0, keepdims=True)
    inv_std = lax.rsqrt(jnp.mean(centre * centre, axis=0, keepdims=True) + 1e-05)
    return centre * inv_std, inv_std


def forward_kernel(
    pair_ref, bucket_ref, gain_ref, w_in_ref, b_in_ref, w_out_ref, table_ref, pre_ref, bias_ref, w_pre, w_mix, table,
    gain, *, group, merge
):
    rows, chans, keys = pair_ref.shape
    heads, buckets = table_ref.shape
    width = merge * keys
    first_row = pl.program_id(0) * rows

    @pl.when(pl.program_id(0) == 0)
    def _():
        stacked = jnp.concatenate([w_in_ref[...], as_rows(split_low(b_in_ref[...], 3), ROWS)], axis=0)
        w_pre[...] = transposed(stacked).astype(BF16)
        w_mix[...] = (w_out_ref[...].astype(F32) * 0.5).astype(BF16)
        place = jnp.where(
            lax.broadcasted_iota(jnp.int32, (buckets, LANES), 0) == lax.broadcasted_iota(jnp.int32, (buckets, LANES), 1),
            1.0,
            0.0,
        ).astype(BF16)
        table[...] = jnp.dot(table_ref[...], place, preferred_element_type=F32)
        gain[...] = gain_columns(gain_ref[...])

    def some_rows(row):
        pairs = jnp.concatenate([pair_ref[row + member] for member in range(merge)], axis=1)
        unit_pairs, _ = unit_norm(pairs.astype(F32))
        normed = (unit_pairs * widen(gain[...], width)).astype(BF16)
        ones = jnp.where(lax.broadcasted_iota(jnp.int32, (ROWS, width), 0) < 3, 1.0, 0.0).astype(BF16)
        pre_act = jnp.dot(w_pre[...], jnp.concatenate([normed, ones], axis=0), preferred_element_type=F32)
        hidden = (pre_act * (lax.erf(pre_act * RSQRT2) + 1.0)).astype(BF16)
        pre_low = pre_act.astype(BF16)
        outs = []
        mixed = jnp.dot(w_mix[...], hidden, preferred_element_type=F32)
        for member in range(merge):
            pieces = []
            id_row = bucket_ref[pl.ds(first_row + row + member, 1), :]
            for part in range(keys // LANES):
                begin = member * keys + part * LANES
                pre_ref[row + member, part] = pre_low[:, begin : begin + LANES]
                ids = id_row[:, part * LANES : (part + 1) * LANES]
                lookup = jnp.take_along_axis(table[...], jnp.broadcast_to(ids, (heads, LANES)), axis=1)
                pieces.append(mixed[:, begin : begin + LANES] + lookup)
            outs.append(jnp.concatenate(pieces, axis=1))
        return outs

    def step(index, carry):
        outs = []
        for member in range(0, group, merge):
            outs += some_rows(index * group + member)
        size = group * heads
        bias_ref[pl.ds(pl.multiple_of(index * size, size), size), :] = jnp.concatenate(outs, axis=0).astype(BF16)
        return carry

    lax.fori_loop(0, rows // group, step, 0)


def forward_call(pair_feats, bucket_ids, gain, w_in, b_in, w_out, table):
    rows, chans, keys = pair_feats.shape
    heads, hid = w_out.shape
    block = divisor(rows, 8)
    parts = keys // LANES
    return pl.pallas_call(
        functools.partial(forward_kernel, group=block, merge=divisor(block, 2)),
        grid=(rows // block,),
        in_specs=[
            pl.BlockSpec((block, chans, keys), lambda i: (i, 0, 0)),
            full_spec(bucket_ids),
            full_spec(gain),
            full_spec(w_in),
            full_spec(b_in),
            full_spec(w_out),
            full_spec(table),
        ],
        out_specs=[
            pl.BlockSpec((block, parts, hid, LANES), lambda i: (i, 0, 0, 0)),
            pl.BlockSpec((block * heads, keys), lambda i: (i, 0)),
        ],
        out_shape=[
            jax.ShapeDtypeStruct((rows, parts, hid, LANES), BF16),
            jax.ShapeDtypeStruct((rows * heads, keys), BF16),
        ],
        scratch_shapes=[
            pltpu.VMEM((hid, chans + ROWS), BF16),
            pltpu.VMEM((heads, hid), BF16),
            pltpu.VMEM((heads, LANES), F32),
            pltpu.VMEM((chans, LANES), F32),
        ],
        compiler_params=pltpu.CompilerParams(vmem_limit_bytes=FULL_LIMIT),
        cost_estimate=pl.CostEstimate(
            flops=2 * rows * keys * hid * 256,
            bytes_accessed=2 * rows * keys * (hid + chans),
            transcendentals=2 * rows * keys * hid,
        ),
        name="pair_forward",
    )(pair_feats, bucket_ids, gain, w_in, b_in, w_out, table)


def attention_kernel(
    bias_ref, kv_ref, aux_ref, mask_ref, ds_ref, part_ref, q_rows, d_rows, q_cols, d_cols, norm_ref, delta_ref,
    dq_acc, *, head_dim, rows
):
    heads = kv_ref.shape[0]
    tile = bias_ref.shape[1]
    width = heads * head_dim
    flat = rows * heads
    scale = 1.0 / math.sqrt(head_dim)
    step = pl.program_id(0)
    cols = pl.ds(pl.multiple_of(step * tile, tile), tile)
    offset = lax.rem(lax.axis_index("heads") * rows, LANES)
    scalar_offset = lax.rem(offset + LANES // 2, LANES)

    def spread_matrix():
        lane = lax.broadcasted_iota(jnp.int32, (flat, LANES), 1)
        return lane == lax.broadcasted_iota(jnp.int32, (flat, LANES), 0) // heads + offset

    def own_columns():
        return (
            lax.broadcasted_iota(jnp.int32, (width, flat), 1) % heads
            == lax.broadcasted_iota(jnp.int32, (width, flat), 0) // head_dim
        )

    @pl.when(step == 0)
    def _():
        spread_low = jnp.where(spread_matrix(), 1.0, 0.0).astype(BF16)
        own_rows = (
            lax.broadcasted_iota(jnp.int32, (flat, width), 0) % heads
            == lax.broadcasted_iota(jnp.int32, (flat, width), 1) // head_dim
        )
        own_cols = own_columns()
        for begin, by_rows, by_cols in ((0, q_rows, q_cols), (head_dim, d_rows, d_cols)):
            block = aux_ref[:, begin : begin + head_dim, :].reshape(width, LANES)
            spread = lax.dot_general(spread_low, block, NT, preferred_element_type=F32)
            by_rows[...] = jnp.where(own_rows, spread, 0.0).astype(BF16)
            spread = lax.dot_general(block, spread_low, NT, preferred_element_type=F32)
            by_cols[...] = jnp.where(own_cols, spread, 0.0).astype(BF16)
        tail = aux_ref[:, :ROWS, :].astype(F32)
        lane = lax.broadcasted_iota(jnp.int32, (rows, heads, LANES), 2)
        own_lane = lane == lax.broadcasted_iota(jnp.int32, (rows, heads, LANES), 0) + scalar_offset
        for begin, target in ((0, norm_ref), (3, delta_ref)):
            pieces = tail[:, begin, :] + tail[:, begin + 1, :] + tail[:, begin + 2, :]
            column = jnp.sum(jnp.where(own_lane, pieces[None], 0.0), axis=2, keepdims=True)
            target[...] = jnp.broadcast_to(column.reshape(flat, 1), target.shape)
        dq_acc[...] = jnp.zeros_like(dq_acc)

    norm = widen(norm_ref[...], tile)
    delta = widen(delta_ref[...], tile)
    keys = kv_ref[:, :head_dim, :].reshape(width, tile)
    values = kv_ref[:, head_dim:, :].reshape(width, tile)
    scores = jnp.dot(q_rows[...], keys, preferred_element_type=F32) * scale + bias_ref[...].astype(F32)
    probs = jnp.where(mask_ref[...] == 1, jnp.exp(scores - norm), 0.0)
    dprobs = jnp.dot(d_rows[...], values, preferred_element_type=F32)
    dscores = (probs * (dprobs - delta)).astype(BF16)
    ds_ref[...] = dscores
    dk_part = jnp.dot(q_cols[...], dscores, preferred_element_type=F32)
    dv_part = jnp.dot(d_cols[...], probs.astype(BF16), preferred_element_type=F32)
    part_ref[:, :head_dim, cols] = dk_part.reshape(heads, head_dim, tile).astype(BF16)
    part_ref[:, head_dim : 2 * head_dim, cols] = dv_part.reshape(heads, head_dim, tile).astype(BF16)
    dq_acc[...] += lax.dot_general(keys, dscores, NT, preferred_element_type=F32)

    @pl.when(step == pl.num_programs(0) - 1)
    def _():
        spread_low = jnp.where(spread_matrix(), 1.0, 0.0).astype(BF16)
        total = None
        for piece in split_low(jnp.where(own_columns(), dq_acc[...], 0.0), 3):
            part = jnp.dot(piece.astype(BF16), spread_low, preferred_element_type=F32)
            total = part if total is None else total + part
        high, rest = split_low(total, 2)
        keys_end = part_ref.shape[2] - LANES
        part_ref[:, :head_dim, keys_end:] = high.astype(BF16).reshape(heads, head_dim, LANES)
        part_ref[:, head_dim:, keys_end:] = rest.astype(BF16).reshape(heads, head_dim, LANES)


def attention_call(bias, received, key_mask, head_dim, rows):
    flat, keys = bias.shape
    heads, depth, _ = received.shape
    width = heads * head_dim
    tile = divisor(keys, 256)
    return pl.pallas_call(
        functools.partial(attention_kernel, head_dim=head_dim, rows=rows),
        grid=(keys // tile,),
        in_specs=[
            pl.BlockSpec((flat, tile), lambda i: (0, i)),
            pl.BlockSpec((heads, 2 * head_dim, tile), lambda i: (0, 0, i)),
            pl.BlockSpec((heads, depth, LANES), lambda i: (0, 0, keys // LANES)),
            pl.BlockSpec((1, tile), lambda i: (0, i)),
        ],
        out_specs=[
            pl.BlockSpec((flat, tile), lambda i: (0, i)),
            pl.BlockSpec((heads, depth, keys + LANES), lambda i: (0, 0, 0)),
        ],
        out_shape=[
            jax.ShapeDtypeStruct((flat, keys), BF16),
            jax.ShapeDtypeStruct((heads, depth, keys + LANES), BF16),
        ],
        scratch_shapes=[
            pltpu.VMEM((flat, width), BF16),
            pltpu.VMEM((flat, width), BF16),
            pltpu.VMEM((width, flat), BF16),
            pltpu.VMEM((width, flat), BF16),
            pltpu.VMEM((flat, LANES), F32),
            pltpu.VMEM((flat, LANES), F32),
            pltpu.VMEM((width, flat), F32),
        ],
        compiler_params=pltpu.CompilerParams(vmem_limit_bytes=BIG_LIMIT),
        cost_estimate=pl.CostEstimate(
            flops=10 * flat * keys * width, bytes_accessed=8 * flat * keys, transcendentals=flat * keys
        ),
        name="pair_attention",
    )(bias, received, received, key_mask.reshape(1, keys))


def backward_kernel(pair_ref, ds_ref, pre_ref, gain_ref, w_in_ref, w_out_ref, *rest, group):
    out_ref, w_back, gain = rest[-3:]
    rows, chans, keys = pair_ref.shape
    heads = w_out_ref.shape[0]
    parts = keys // LANES

    @pl.when(pl.program_id(0) == 0)
    def _():
        w_back[...] = (transposed(w_out_ref[...]) * 0.5).astype(BF16)
        gain[...] = gain_columns(gain_ref[...])

    def step(index, carry):
        size = group * heads
        dscores = ds_ref[pl.ds(pl.multiple_of(index * size, size), size), :]
        for member in range(group):
            row = index * group + member
            unit_pairs, inv_std = unit_norm(pair_ref[row].astype(F32))
            pre_act = jnp.concatenate([pre_ref[row, part] for part in range(parts)], axis=1)
            dhidden = jnp.dot(
                w_back[...], dscores[member * heads : (member + 1) * heads], preferred_element_type=F32
            )
            cdf2 = lax.erf(pre_act * low(RSQRT2)) + low(1.0)
            density2 = jnp.exp2(pre_act * pre_act * low(EXP2_SCALE) + low(EXP2_SHIFT))
            dpre = dhidden.astype(BF16) * (cdf2 + pre_act * density2)
            dunit = jnp.dot(w_in_ref[...], dpre, preferred_element_type=F32) * widen(gain[...], keys)
            first_mean = jnp.mean(dunit, axis=0, keepdims=True)
            second_mean = jnp.mean(dunit * unit_pairs, axis=0, keepdims=True)
            out_ref[row] = (inv_std * (dunit - first_mean - unit_pairs * second_mean)).astype(BF16)
        return carry

    lax.fori_loop(0, rows // group, step, 0)


def backward_call(pair_feats, dscores, pre_act, gain, w_in, w_out, begin, count, previous):
    rows, chans, keys = pair_feats.shape
    parts = keys // LANES
    heads, hid = w_out.shape
    block = divisor(math.gcd(begin, count), 8)
    first = begin // block
    operands = [pair_feats, dscores, pre_act, gain, w_in, w_out]
    in_specs = [
        pl.BlockSpec((block, chans, keys), lambda i: (i + first, 0, 0)),
        pl.BlockSpec((block * heads, keys), lambda i: (i + first, 0)),
        pl.BlockSpec((block, parts, hid, LANES), lambda i: (i + first, 0, 0, 0)),
        full_spec(gain),
        full_spec(w_in),
        full_spec(w_out),
    ]
    aliases = {}
    if previous is not None:
        aliases = {len(operands): 0}
        operands.append(previous)
        in_specs.append(pl.BlockSpec(memory_space=pl.ANY))
    return pl.pallas_call(
        functools.partial(backward_kernel, group=block),
        grid=(count // block,),
        in_specs=in_specs,
        out_specs=pl.BlockSpec((block, chans, keys), lambda i: (i + first, 0, 0)),
        out_shape=jax.ShapeDtypeStruct((rows, chans, keys), BF16),
        scratch_shapes=[pltpu.VMEM((hid, heads), BF16), pltpu.VMEM((chans, LANES), F32)],
        input_output_aliases=aliases,
        compiler_params=pltpu.CompilerParams(vmem_limit_bytes=FULL_LIMIT),
        cost_estimate=pl.CostEstimate(
            flops=2 * count * keys * hid * 256,
            bytes_accessed=2 * count * keys * (hid + 2 * chans),
            transcendentals=0,
        ),
        name="pair_backward",
    )(*operands)


def sum_kernel(part_ref, dkv_ref, dq_ref, *, head_dim, rows):
    sources, own_heads, _, lanes = part_ref.shape
    keys = lanes - LANES
    for head in range(own_heads):
        total = part_ref[0, head, :, :keys].astype(F32)
        for source in range(1, sources):
            total = total + part_ref[source, head, :, :keys].astype(F32)
        dkv_ref[head] = total
        dq_ref[head] = jnp.zeros(dq_ref.shape[1:], F32)
        for source in range(sources):
            slab = source * rows // LANES * LANES
            piece = part_ref[source, head, :, keys:].astype(F32)
            dq_ref[head, :, slab : slab + LANES] += piece[:head_dim] + piece[head_dim:]


def sum_call(parts, head_dim, rows, queries):
    _, own_heads, _, lanes = parts.shape
    return pl.pallas_call(
        functools.partial(sum_kernel, head_dim=head_dim, rows=rows),
        out_shape=[
            jax.ShapeDtypeStruct((own_heads, 2 * head_dim, lanes - LANES), F32),
            jax.ShapeDtypeStruct((own_heads, head_dim, queries), F32),
        ],
        compiler_params=pltpu.CompilerParams(vmem_limit_bytes=SMALL_LIMIT),
        name="sum_sources",
    )(parts)


def finish_kernel(dkv_ref, dkv_other, dq_ref, dq_other, grad_q, grad_k, grad_v, *, head_dim):
    scale = 1.0 / math.sqrt(head_dim)
    total = dkv_ref[...] + dkv_other[...]
    grad_q[...] = ((dq_ref[...] + dq_other[...]) * scale).astype(BF16)
    grad_k[...] = (total[:, :head_dim, :] * scale).astype(BF16)
    grad_v[...] = total[:, head_dim:, :].astype(BF16)


def finish_call(dkv, dkv_other, dq, dq_other):
    own_heads, head_dim, queries = dq.shape
    keys = dkv.shape[2]
    return pl.pallas_call(
        functools.partial(finish_kernel, head_dim=head_dim),
        out_shape=[
            jax.ShapeDtypeStruct((own_heads, head_dim, queries), BF16),
            jax.ShapeDtypeStruct((own_heads, head_dim, keys), BF16),
            jax.ShapeDtypeStruct((own_heads, head_dim, keys), BF16),
        ],
        compiler_params=pltpu.CompilerParams(vmem_limit_bytes=SMALL_LIMIT),
        name="finish",
    )(dkv, dkv_other, dq, dq_other)


def per_device(
    pair_feats,
    bucket_ids,
    ln_gain,
    w_in,
    b_in,
    w_out,
    bucket_table,
    key_mask,
    q_heads,
    k_heads,
    v_heads,
    out_heads,
    dout_heads,
    log_norm,
):
    axis_size = lax.axis_size("heads")
    own_heads, head_dim, queries = q_heads.shape
    rows = pair_feats.shape[0]
    gain = ln_gain.reshape(1, -1)

    packed = pack_call(k_heads, v_heads, q_heads, dout_heads, out_heads, log_norm, axis_size, rows)
    received = lax.all_to_all(packed, "heads", split_axis=0, concat_axis=0, tiled=True)
    pre_act, bias_vals = forward_call(
        pair_feats, bucket_ids, gain, w_in, b_in.reshape(1, -1), w_out.T, bucket_table.T
    )
    received = received.reshape((axis_size * own_heads,) + received.shape[2:])
    dscores, parts = attention_call(bias_vals, received, key_mask, head_dim, rows)
    parts = lax.all_to_all(
        parts.reshape((axis_size, own_heads) + parts.shape[1:]), "heads", split_axis=0, concat_axis=0, tiled=True
    )
    last = 8
    weights = (gain, w_in, w_out.T)
    grad_pairs = backward_call(pair_feats, dscores, pre_act, *weights, 0, rows - last, None)
    parts, grad_pairs = lax.optimization_barrier((parts, grad_pairs))
    dkv_sum, dq_sum = sum_call(parts, head_dim, rows, queries)
    grad_pairs, dkv_sum, dq_sum = lax.optimization_barrier((grad_pairs, dkv_sum, dq_sum))
    dkv_other = other_sum(dkv_sum, "query")
    dq_other = other_sum(dq_sum, "key")
    grad_pairs = backward_call(pair_feats, dscores, pre_act, *weights, rows - last, last, grad_pairs)
    grad_q, grad_k, grad_v = finish_call(dkv_sum, dkv_other, dq_sum, dq_other)
    return (grad_pairs, grad_q, grad_k, grad_v)


def solution(mesh):
    def traced(*args):
        with jax.sharding.use_abstract_mesh(mesh.abstract_mesh):
            return jax.shard_map(
                per_device,
                mesh=mesh,
                in_specs=(
                    P(("query", "heads"), None, "key"),
                    P(("query", "heads"), "key"),
                    P(),
                    P(),
                    P(),
                    P(),
                    P(),
                    P("key"),
                    P("heads", None, "query"),
                    P("heads", None, "key"),
                    P("heads", None, "key"),
                    P("heads", None, "query"),
                    P("heads", None, "query"),
                    P("heads", "query"),
                ),
                out_specs=(
                    P(("query", "heads"), None, "key"),
                    P("heads", None, "query"),
                    P("heads", None, "key"),
                    P("heads", None, "key"),
                ),
                check_vma=False,
            )(*args)

    return traced
```

time: 131 us -> 91.3 us (0.70)
  Pallas kernels: 106 us -> 70.5 us
  local copies, waits for them, and re-layouts: 6.18 us -> 2.2 us
  starting transfers between devices: 14.8 us -> 12.7 us
  waiting for transfers between devices: 2.89 us -> 4.91 us
    pallas_call x3, Pallas kernels: 93.8 us -> 62.5 us  [the longest x2 38.8 us: backward_call(): pl.pallas_call(functools.partial(backward_kernel, group=block), grid=(cou...]
    all_to_all x1, waiting for transfers between devices: 0.01 us -> 4.9 us  [per_device(): lax.all_to_all(packed, 'heads', split_axis=0, concat_axis=0, tiled=True)]
    unnamed x10 -> x6, local copies, waits for them, and re-layouts: 6.18 us -> 2.2 us
    all_to_all x1, waiting for transfers between devices: 2.88 us -> 0.01 us  [per_device(): lax.all_to_all(parts.reshape((axis_size, own_heads) + parts.shape[1:]), '...]
    all_to_all x1, starting transfers between devices: 6 us -> 3.74 us  [per_device(): lax.all_to_all(parts.reshape((axis_size, own_heads) + parts.shape[1:]), '...]
    pallas_call x1, Pallas kernels: 2.21 us -> 0.19 us  [sum_call(): pl.pallas_call(functools.partial(sum_kernel, head_dim=head_dim, rows=rows...]
    pallas_call x1, Pallas kernels: 6.42 us -> 5.1 us  [attention_call(): pl.pallas_call(functools.partial(attention_kernel, head_dim=head_dim, row...]
  transfers between devices with their start and end apart: 4 -> 4, of which waited for: 1 -> 1; matrix products, arithmetic and copies ran while one was open for 2% -> 0% of each run, Pallas kernels for 72% -> 69%
where the time goes in v3:
time: 91.3 us; the launch traced here: 91 us
  Pallas kernels  70.5 us (77%)
  starting transfers between devices  12.7 us (14%)
  waiting for transfers between devices  4.91 us (5%)
  local copies, waits for them, and re-layouts  2.2 us (2%)
    pallas_call x2, Pallas kernels, backward_call(): pl.pallas_call(functools.partial(backward_kernel, group=block), grid=(cou...  38.8 us
    pallas_call x1, Pallas kernels, forward_call(): pl.pallas_call(functools.partial(forward_kernel, group=block, merge=divis...  23.7 us
    all_to_all x1, starting transfers between devices, per_device(): lax.all_to_all(packed, 'heads', split_axis=0, concat_axis=0, tiled=True)  7.31 us
    pallas_call x1, Pallas kernels, attention_call(): pl.pallas_call(functools.partial(attention_kernel, head_dim=head_dim, row...  5.1 us
    all_to_all x1, waiting for transfers between devices, per_device(): lax.all_to_all(packed, 'heads', split_axis=0, concat_axis=0, tiled=True)  4.9 us
    all_to_all x1, starting transfers between devices, per_device(): lax.all_to_all(parts.reshape((axis_size, own_heads) + parts.shape[1:]), '...  3.74 us
    unnamed x6, local copies, waits for them, and re-layouts  2.2 us
    pallas_call x1, Pallas kernels, pack_call(): pl.pallas_call(functools.partial(pack_kernel, rows=rows), out_shape=jax.S...  2.02 us
  transfers between devices with their start and end apart: 4, of which 1 were waited for; matrix products, arithmetic and copies ran while one was open for 0% of the time, Pallas kernels for 69%

profile of v3, /device:TPU:0, one launch (start us, length us, event | category | flops | bytes accessed | tf_op | source)
XLA Modules:
  0.0 91.0 jit_solution(4182478825911105936)
XLA Ops:
  0.6 2.0 %pack_heads.1 = bf16[8,1,64,1152]{3,2,1,0:T(8,128)(2,1)} custom-call(bf16[1,32,1024]{2,1,0:T(8,128)(2,1)} %k_ref.1, bf16[1,32,1024]{2,1,0:T(8,128)(2,1)} %v_ref.1, bf16[1,32,512]{2,1,0:T(8,128)(2,1)} %q_ref.1, bf16[1,32,512]{2,1,0:T(8,128)(2,1)} %dout_ref.1, bf16[1,32,512]{2,1,0:T(8,128)(2,1)} %out_ref.1, f32[1,512]{1,0:T(1,128)} %norm_ref.1), custom_call_target="tpu_custom_call" | custom-call | tf_op jit(solution)/shard_map/pack_heads/pallas_call | solution.py:105
  2.7 7.3 %all-to-all-start = ((bf16[8,1,64,1152]{3,2,1,0:T(8,128)(2,1)}), bf16[8,1,64,1152]{3,2,1,0:T(8,128)(2,1)S(1)}, u32[]{:S(2)}, u32[]{:S(2)}) async-start(bf16[8,1,64,1152]{3,2,1,0:T(8,128)(2,1)} %pack_heads.1), calls=%async_computation | async-start | bytes 2359296 | tf_op jit(solution)/shard_map/all_to_all | solution.py:473
  10.0 0.0 copy-start.1
  10.0 23.7 %pair_forward.1 = (bf16[64,8,256,128]{3,2,1,0:T(8,128)(2,1)}, bf16[512,1024]{1,0:T(8,128)(2,1)}) custom-call(bf16[64,64,1024]{2,1,0:T(8,128)(2,1)} %pair_ref.5, s32[64,1024]{1,0:T(8,128)} %bucket_ref.1, f32[1,64]{1,0:T(1,128)} %bitcast.13, bf16[64,256]{1,0:T(8,128)(2,1)} %w_in_ref.5, f32[1,256]{1,0:T(1,128)} %bitcast.17, bf16[8,256]{1,0:T(8,128)(2,1)} %bitcast.10, ...), custom_call_target="tpu_custom_call" | custom-call | flops 8589934592 | bytes 41943040 | tf_op jit(solution)/shard_map/pair_forward/pallas_call | solution.py:179
  33.6 4.9 %all-to-all-done = bf16[8,1,64,1152]{3,2,1,0:T(8,128)(2,1)S(1)} async-done(((bf16[8,1,64,1152]{3,2,1,0:T(8,128)(2,1)}), bf16[8,1,64,1152]{3,2,1,0:T(8,128)(2,1)S(1)}, u32[]{:S(2)}, u32[]{:S(2)}) %all-to-all-start) | async-done | bytes 1179680 | tf_op jit(solution)/shard_map/all_to_all | solution.py:473
  38.5 0.0 copy-done.1
  38.5 0.0 copy-start.2
  38.5 1.2 %copy-done.2 = bf16[512,1024]{1,0:T(8,128)(2,1)S(1)} copy-done((bf16[512,1024]{1,0:T(8,128)(2,1)S(1)}, bf16[512,1024]{1,0:T(8,128)(2,1)}, u32[]{:S(2)}) %copy-start.2) | copy-done | bytes 1048600
  39.8 5.1 %pair_attention.1 = (bf16[512,1024]{1,0:T(8,128)(2,1)S(1)}, bf16[8,64,1152]{2,1,0:T(8,128)(2,1)}) custom-call(bf16[512,1024]{1,0:T(8,128)(2,1)S(1)} %copy-done.2, bf16[8,64,1152]{2,1,0:T(8,128)(2,1)S(1)} %bitcast.7, bf16[8,64,1152]{2,1,0:T(8,128)(2,1)S(1)} %bitcast.8, s32[1,1024]{1,0:T(1,128)S(1)} %bitcast.9), custom_call_target="tpu_custom_call" | custom-call | flops 1342177280 | bytes 4194304 | tf_op jit(solution)/shard_map/pair_attention/pallas_call | solution.py:295
  44.9 0.0 copy-start
  44.9 1.0 %copy-done = bf16[512,1024]{1,0:T(8,128)(2,1)} copy-done((bf16[512,1024]{1,0:T(8,128)(2,1)}, bf16[512,1024]{1,0:T(8,128)(2,1)S(1)}, u32[]{:S(2)}) %copy-start) | copy-done | bytes 1048600
  45.9 3.7 %all-to-all-start.1 = ((bf16[8,1,64,1152]{3,2,1,0:T(8,128)(2,1)}), bf16[8,1,64,1152]{3,2,1,0:T(8,128)(2,1)S(1)}, u32[]{:S(2)}, u32[]{:S(2)}) async-start(bf16[8,1,64,1152]{3,2,1,0:T(8,128)(2,1)} %bitcast.6), calls=%async_computation.1 | async-start | bytes 2359296 | tf_op jit(solution)/shard_map/all_to_all | solution.py:479
  49.6 31.5 %pair_backward.2.rest_0_ = bf16[64,64,1024]{2,1,0:T(8,128)(2,1)} custom-call(bf16[64,64,1024]{2,1,0:T(8,128)(2,1)} %pair_ref.5, bf16[512,1024]{1,0:T(8,128)(2,1)} %copy-done, bf16[64,8,256,128]{3,2,1,0:T(8,128)(2,1)} %get-tuple-element.20.pre_ref, f32[1,64]{1,0:T(1,128)} %bitcast.14, bf16[64,256]{1,0:T(8,128)(2,1)} %w_in_ref.5, bf16[8,256]{1,0:T(8,128)(2,1)} %bitcast.11), custom_call_target="tpu_custom_call" | custom-call | flops 7516192768 | bytes 44040192 | tf_op jit(solution)/shard_map/pair_backward/pallas_call | solution.py:382
  81.1 0.0 all-to-all-done.1.part_ref
  81.1 0.2 sum_sources.1
  81.3 0.1 collective-permute-start
  81.4 1.6 %collective-permute-start.1 = (f32[1,32,512]{2,1,0:T(8,128)S(1)}, f32[1,32,512]{2,1,0:T(8,128)S(1)}, u32[]{:S(2)}, u32[]{:S(2)}) collective-permute-start(f32[1,32,512]{2,1,0:T(8,128)S(1)} %get-tuple-element.28.dq_ref), channel_id=1, source_target_pairs={{0,8},{8,0},{1,9},{9,1},{2,10},{10,2},{3,11},{11,3},{4,12},{12,4},... | collective-permute-start | bytes 196616 | tf_op jit(solution)/shard_map/ppermute | solution.py:78
  82.9 7.3 %pair_backward.3 = bf16[64,64,1024]{2,1,0:T(8,128)(2,1)} custom-call(bf16[64,64,1024]{2,1,0:T(8,128)(2,1)} %pair_ref.5, bf16[512,1024]{1,0:T(8,128)(2,1)} %copy-done, bf16[64,8,256,128]{3,2,1,0:T(8,128)(2,1)} %get-tuple-element.20.pre_ref, f32[1,64]{1,0:T(1,128)} %bitcast.15, bf16[64,256]{1,0:T(8,128)(2,1)} %w_in_ref.5, ...), custom_call_target="tpu_custom_call", output_to_operand_aliasing={{}: (6, {})} | custom-call | flops 1073741824 | bytes 6291456 | tf_op jit(solution)/shard_map/pair_backward/pallas_call | solution.py:382
  90.3 0.0 collective-permute-done.1.dq_other
  90.3 0.0 collective-permute-done.dkv_other
  90.3 0.7 finish.1
Async XLA Ops:
  2.7 35.9 %all-to-all-start = ((bf16[8,1,64,1152]{3,2,1,0:T(8,128)(2,1)}), bf16[8,1,64,1152]{3,2,1,0:T(8,128)(2,1)S(1)}, u32[]{:S(2)}, u32[]{:S(2)}) async-start(bf16[8,1,64,1152]{3,2,1,0:T(8,128)(2,1)} %pack_heads.1), calls=%async_computation | async-start | bytes 2359296 | tf_op jit(solution)/shard_map/all_to_all | solution.py:473
  10.0 28.6 %copy-start.1 = (s32[1024]{0:T(1024)S(1)}, s32[1024]{0:T(1024)}, u32[]{:S(2)}) copy-start(s32[1024]{0:T(1024)} %param.21) | copy-start | bytes 12292
  38.5 1.2 %copy-start.2 = (bf16[512,1024]{1,0:T(8,128)(2,1)S(1)}, bf16[512,1024]{1,0:T(8,128)(2,1)}, u32[]{:S(2)}) copy-start(bf16[512,1024]{1,0:T(8,128)(2,1)} %get-tuple-element.18.bias_ref) | copy-start | bytes 3145732
  44.9 1.0 %copy-start = (bf16[512,1024]{1,0:T(8,128)(2,1)}, bf16[512,1024]{1,0:T(8,128)(2,1)S(1)}, u32[]{:S(2)}) copy-start(bf16[512,1024]{1,0:T(8,128)(2,1)S(1)} %get-tuple-element.19.ds_ref) | copy-start | bytes 3145732
  45.9 35.3 %all-to-all-start.1 = ((bf16[8,1,64,1152]{3,2,1,0:T(8,128)(2,1)}), bf16[8,1,64,1152]{3,2,1,0:T(8,128)(2,1)S(1)}, u32[]{:S(2)}, u32[]{:S(2)}) async-start(bf16[8,1,64,1152]{3,2,1,0:T(8,128)(2,1)} %bitcast.6), calls=%async_computation.1 | async-start | bytes 2359296 | tf_op jit(solution)/shard_map/all_to_all | solution.py:479
  81.3 9.0 %collective-permute-start = (f32[1,64,1024]{2,1,0:T(8,128)S(1)}, f32[1,64,1024]{2,1,0:T(8,128)S(1)}, u32[]{:S(2)}, u32[]{:S(2)}) collective-permute-start(f32[1,64,1024]{2,1,0:T(8,128)S(1)} %get-tuple-element.27.dkv_ref), channel_id=1, source_target_pairs={{0,16},{16,0},{1,17},{17,1},{2,18},{18,2},{3,19},{19,3},{4,20},{20... | collective-permute-start | bytes 786440 | tf_op jit(solution)/shard_map/ppermute | solution.py:78
  81.4 8.9 %collective-permute-start.1 = (f32[1,32,512]{2,1,0:T(8,128)S(1)}, f32[1,32,512]{2,1,0:T(8,128)S(1)}, u32[]{:S(2)}, u32[]{:S(2)}) collective-permute-start(f32[1,32,512]{2,1,0:T(8,128)S(1)} %get-tuple-element.28.dq_ref), channel_id=1, source_target_pairs={{0,8},{8,0},{1,9},{9,1},{2,10},{10,2},{3,11},{11,3},{4,12},{12,4},... | collective-permute-start | bytes 196616 | tf_op jit(solution)/shard_map/ppermute | solution.py:78

commit v4 on v3

--- a/solution.py
+++ b/solution.py
@@ -11,8 +11,8 @@
 F32 = jnp.float32
 BF16 = jnp.bfloat16
 RSQRT2 = 1.0 / math.sqrt(2.0)
-EXP2_SCALE = -0.5 / math.log(2.0)
-EXP2_SHIFT = math.log2(2.0 / math.sqrt(2.0 * math.pi))
+EXP2_SCALE = -1.0 / math.log(2.0)
+EXP2_SHIFT = math.log2(2.0 / math.sqrt(math.pi))
 ROWS = 16
 LANES = 128
 NT = (((1,), (1,)), ((), ()))
@@ -117,8 +117,8 @@
 
 
 def forward_kernel(
-    pair_ref, bucket_ref, gain_ref, w_in_ref, b_in_ref, w_out_ref, table_ref, pre_ref, bias_ref, w_pre, w_mix, table,
-    gain, *, group, merge
+    pair_ref, bucket_ref, gain_ref, w_in_ref, b_in_ref, w_out_ref, table_ref, scaled_ref, unit_ref, inv_ref, bias_ref, w_pre,
+    w_mix, table, gain, *, group, merge
 ):
     rows, chans, keys = pair_ref.shape
     heads, buckets = table_ref.shape
@@ -140,20 +140,24 @@
 
     def some_rows(row):
         pairs = jnp.concatenate([pair_ref[row + member] for member in range(merge)], axis=1)
-        unit_pairs, _ = unit_norm(pairs.astype(F32))
+        unit_pairs, inv_std = unit_norm(pairs.astype(F32))
+        unit_low = unit_pairs.astype(BF16)
         normed = (unit_pairs * widen(gain[...], width)).astype(BF16)
         ones = jnp.where(lax.broadcasted_iota(jnp.int32, (ROWS, width), 0) < 3, 1.0, 0.0).astype(BF16)
         pre_act = jnp.dot(w_pre[...], jnp.concatenate([normed, ones], axis=0), preferred_element_type=F32)
-        hidden = (pre_act * (lax.erf(pre_act * RSQRT2) + 1.0)).astype(BF16)
-        pre_low = pre_act.astype(BF16)
+        scaled = pre_act * RSQRT2
+        hidden = (pre_act * (lax.erf(scaled) + 1.0)).astype(BF16)
+        scaled_low = scaled.astype(BF16)
         outs = []
         mixed = jnp.dot(w_mix[...], hidden, preferred_element_type=F32)
         for member in range(merge):
             pieces = []
+            inv_ref[pl.ds(row + member, 1), :] = inv_std[:, member * keys : (member + 1) * keys]
             id_row = bucket_ref[pl.ds(first_row + row + member, 1), :]
             for part in range(keys // LANES):
                 begin = member * keys + part * LANES
-                pre_ref[row + member, part] = pre_low[:, begin : begin + LANES]
+                scaled_ref[row + member, part] = scaled_low[:, begin : begin + LANES]
+                unit_ref[row + member, part] = unit_low[:, begin : begin + LANES]
                 ids = id_row[:, part * LANES : (part + 1) * LANES]
                 lookup = jnp.take_along_axis(table[...], jnp.broadcast_to(ids, (heads, LANES)), axis=1)
                 pieces.append(mixed[:, begin : begin + LANES] + lookup)
@@ -190,10 +194,14 @@
         ],
         out_specs=[
             pl.BlockSpec((block, parts, hid, LANES), lambda i: (i, 0, 0, 0)),
+            pl.BlockSpec((block, parts, chans, LANES), lambda i: (i, 0, 0, 0)),
+            pl.BlockSpec((block, keys), lambda i: (i, 0)),
             pl.BlockSpec((block * heads, keys), lambda i: (i, 0)),
         ],
         out_shape=[
             jax.ShapeDtypeStruct((rows, parts, hid, LANES), BF16),
+            jax.ShapeDtypeStruct((rows, parts, chans, LANES), BF16),
+            jax.ShapeDtypeStruct((rows, keys), F32),
             jax.ShapeDtypeStruct((rows * heads, keys), BF16),
         ],
         scratch_shapes=[
@@ -326,11 +334,11 @@
     )(bias, received, received, key_mask.reshape(1, keys))
 
 
-def backward_kernel(pair_ref, ds_ref, pre_ref, gain_ref, w_in_ref, w_out_ref, *rest, group):
+def backward_kernel(unit_ref, inv_ref, ds_ref, scaled_ref, gain_ref, w_in_ref, w_out_ref, *rest, group, merge):
     out_ref, w_back, gain = rest[-3:]
-    rows, chans, keys = pair_ref.shape
+    rows, parts, chans, _ = unit_ref.shape
     heads = w_out_ref.shape[0]
-    parts = keys // LANES
+    keys = parts * LANES
 
     @pl.when(pl.program_id(0) == 0)
     def _():
@@ -340,34 +348,38 @@
     def step(index, carry):
         size = group * heads
         dscores = ds_ref[pl.ds(pl.multiple_of(index * size, size), size), :]
-        for member in range(group):
-            row = index * group + member
-            unit_pairs, inv_std = unit_norm(pair_ref[row].astype(F32))
-            pre_act = jnp.concatenate([pre_ref[row, part] for part in range(parts)], axis=1)
-            dhidden = jnp.dot(
-                w_back[...], dscores[member * heads : (member + 1) * heads], preferred_element_type=F32
-            )
-            cdf2 = lax.erf(pre_act * low(RSQRT2)) + low(1.0)
-            density2 = jnp.exp2(pre_act * pre_act * low(EXP2_SCALE) + low(EXP2_SHIFT))
-            dpre = dhidden.astype(BF16) * (cdf2 + pre_act * density2)
-            dunit = jnp.dot(w_in_ref[...], dpre, preferred_element_type=F32) * widen(gain[...], keys)
+        for begin in range(0, group, merge):
+            members = range(begin, begin + merge)
+            tiles = [(index * group + member, part) for member in members for part in range(parts)]
+            unit_pairs = jnp.concatenate([unit_ref[row, part] for row, part in tiles], axis=1).astype(F32)
+            scaled = jnp.concatenate([scaled_ref[row, part] for row, part in tiles], axis=1)
+            inv_std = jnp.concatenate([inv_ref[pl.ds(index * group + member, 1), :] for member in members], axis=1)
+            own = [dscores[member * heads : (member + 1) * heads] for member in members]
+            density2 = jnp.exp2(scaled * scaled * low(EXP2_SCALE) + low(EXP2_SHIFT))
+            slope = lax.erf(scaled) + low(1.0) + scaled * density2
+            dhidden = jnp.dot(w_back[...], jnp.concatenate(own, axis=1), preferred_element_type=F32)
+            dpre = dhidden.astype(BF16) * slope
+            dunit = jnp.dot(w_in_ref[...], dpre, preferred_element_type=F32) * widen(gain[...], keys * merge)
             first_mean = jnp.mean(dunit, axis=0, keepdims=True)
             second_mean = jnp.mean(dunit * unit_pairs, axis=0, keepdims=True)
-            out_ref[row] = (inv_std * (dunit - first_mean - unit_pairs * second_mean)).astype(BF16)
+            grad = (inv_std * (dunit - first_mean - unit_pairs * second_mean)).astype(BF16)
+            for place, member in enumerate(members):
+                out_ref[index * group + member] = grad[:, place * keys : (place + 1) * keys]
         return carry
 
     lax.fori_loop(0, rows // group, step, 0)
 
 
-def backward_call(pair_feats, dscores, pre_act, gain, w_in, w_out, begin, count, previous):
-    rows, chans, keys = pair_feats.shape
-    parts = keys // LANES
+def backward_call(unit_pairs, inv_std, dscores, scaled, gain, w_in, w_out, begin, count, previous):
+    rows, parts, chans, _ = unit_pairs.shape
+    keys = parts * LANES
     heads, hid = w_out.shape
     block = divisor(math.gcd(begin, count), 8)
     first = begin // block
-    operands = [pair_feats, dscores, pre_act, gain, w_in, w_out]
+    operands = [unit_pairs, inv_std, dscores, scaled, gain, w_in, w_out]
     in_specs = [
-        pl.BlockSpec((block, chans, keys), lambda i: (i + first, 0, 0)),
+        pl.BlockSpec((block, parts, chans, LANES), lambda i: (i + first, 0, 0, 0)),
+        pl.BlockSpec((block, keys), lambda i: (i + first, 0)),
         pl.BlockSpec((block * heads, keys), lambda i: (i + first, 0)),
         pl.BlockSpec((block, parts, hid, LANES), lambda i: (i + first, 0, 0, 0)),
         full_spec(gain),
@@ -380,7 +392,7 @@
         operands.append(previous)
         in_specs.append(pl.BlockSpec(memory_space=pl.ANY))
     return pl.pallas_call(
-        functools.partial(backward_kernel, group=block),
+        functools.partial(backward_kernel, group=block, merge=divisor(block, 2)),
         grid=(count // block,),
         in_specs=in_specs,
         out_specs=pl.BlockSpec((block, chans, keys), lambda i: (i + first, 0, 0)),
@@ -471,7 +483,7 @@
 
     packed = pack_call(k_heads, v_heads, q_heads, dout_heads, out_heads, log_norm, axis_size, rows)
     received = lax.all_to_all(packed, "heads", split_axis=0, concat_axis=0, tiled=True)
-    pre_act, bias_vals = forward_call(
+    scaled, unit_pairs, inv_std, bias_vals = forward_call(
         pair_feats, bucket_ids, gain, w_in, b_in.reshape(1, -1), w_out.T, bucket_table.T
     )
     received = received.reshape((axis_size * own_heads,) + received.shape[2:])
@@ -481,13 +493,13 @@
     )
     last = 8
     weights = (gain, w_in, w_out.T)
-    grad_pairs = backward_call(pair_feats, dscores, pre_act, *weights, 0, rows - last, None)
+    grad_pairs = backward_call(unit_pairs, inv_std, dscores, scaled, *weights, 0, rows - last, None)
     parts, grad_pairs = lax.optimization_barrier((parts, grad_pairs))
     dkv_sum, dq_sum = sum_call(parts, head_dim, rows, queries)
     grad_pairs, dkv_sum, dq_sum = lax.optimization_barrier((grad_pairs, dkv_sum, dq_sum))
     dkv_other = other_sum(dkv_sum, "query")
     dq_other = other_sum(dq_sum, "key")
-    grad_pairs = backward_call(pair_feats, dscores, pre_act, *weights, rows - last, last, grad_pairs)
+    grad_pairs = backward_call(unit_pairs, inv_std, dscores, scaled, *weights, rows - last, last, grad_pairs)
     grad_q, grad_k, grad_v = finish_call(dkv_sum, dkv_other, dq_sum, dq_other)
     return (grad_pairs, grad_q, grad_k, grad_v)
 

time: 91.3 us -> 87.9 us (0.963)
  Pallas kernels: 70.5 us -> 66 us
  waiting for transfers between devices: 4.91 us -> 6.05 us
    pallas_call x2, Pallas kernels: 38.8 us -> 34.3 us  [backward_call(): pl.pallas_call(functools.partial(backward_kernel, group=block, merge=divi...]
    all_to_all x1, waiting for transfers between devices: 0.01 us -> 1.22 us  [per_device(): lax.all_to_all(parts.reshape((axis_size, own_heads) + parts.shape[1:]), '...]
  transfers between devices with their start and end apart: 4 -> 4, of which waited for: 1 -> 2; matrix products, arithmetic and copies ran while one was open for 0% -> 0% of each run, Pallas kernels for 69% -> 66%
where the time goes in v4:
time: 87.9 us; the launch traced here: 87.5 us
  Pallas kernels  66 us (75%)
  starting transfers between devices  12.6 us (14%)
  waiting for transfers between devices  6.05 us (7%)
  local copies, waits for them, and re-layouts  2.25 us (3%)
    pallas_call x2, Pallas kernels, backward_call(): pl.pallas_call(functools.partial(backward_kernel, group=block, merge=divi...  34.3 us
    pallas_call x1, Pallas kernels, forward_call(): pl.pallas_call(functools.partial(forward_kernel, group=block, merge=divis...  23.8 us
    all_to_all x1, starting transfers between devices, per_device(): lax.all_to_all(packed, 'heads', split_axis=0, concat_axis=0, tiled=True)  7.31 us
    pallas_call x1, Pallas kernels, attention_call(): pl.pallas_call(functools.partial(attention_kernel, head_dim=head_dim, row...  5.07 us
    all_to_all x1, waiting for transfers between devices, per_device(): lax.all_to_all(packed, 'heads', split_axis=0, concat_axis=0, tiled=True)  4.82 us
    all_to_all x1, starting transfers between devices, per_device(): lax.all_to_all(parts.reshape((axis_size, own_heads) + parts.shape[1:]), '...  3.65 us
    unnamed x6, local copies, waits for them, and re-layouts  2.25 us
    pallas_call x1, Pallas kernels, pack_call(): pl.pallas_call(functools.partial(pack_kernel, rows=rows), out_shape=jax.S...  2.02 us
  transfers between devices with their start and end apart: 4, of which 2 were waited for; matrix products, arithmetic and copies ran while one was open for 0% of the time, Pallas kernels for 66%

profile of v4, /device:TPU:0, one launch (start us, length us, event | category | flops | bytes accessed | tf_op | source)
XLA Modules:
  0.0 87.5 jit_solution(2910239042994213206)
XLA Ops:
  0.6 2.0 %pack_heads.1 = bf16[8,1,64,1152]{3,2,1,0:T(8,128)(2,1)} custom-call(bf16[1,32,1024]{2,1,0:T(8,128)(2,1)} %k_ref.1, bf16[1,32,1024]{2,1,0:T(8,128)(2,1)} %v_ref.1, bf16[1,32,512]{2,1,0:T(8,128)(2,1)} %q_ref.1, bf16[1,32,512]{2,1,0:T(8,128)(2,1)} %dout_ref.1, bf16[1,32,512]{2,1,0:T(8,128)(2,1)} %out_ref.1, f32[1,512]{1,0:T(1,128)} %norm_ref.1), custom_call_target="tpu_custom_call" | custom-call | tf_op jit(solution)/shard_map/pack_heads/pallas_call | solution.py:105
  2.7 7.3 %all-to-all-start = ((bf16[8,1,64,1152]{3,2,1,0:T(8,128)(2,1)}), bf16[8,1,64,1152]{3,2,1,0:T(8,128)(2,1)S(1)}, u32[]{:S(2)}, u32[]{:S(2)}) async-start(bf16[8,1,64,1152]{3,2,1,0:T(8,128)(2,1)} %pack_heads.1), calls=%async_computation | async-start | bytes 2359296 | tf_op jit(solution)/shard_map/all_to_all | solution.py:485
  10.0 0.0 copy-start.1
  10.0 23.8 %pair_forward.1 = (bf16[64,8,256,128]{3,2,1,0:T(8,128)(2,1)}, bf16[64,8,64,128]{3,2,1,0:T(8,128)(2,1)}, f32[64,1024]{1,0:T(8,128)}, bf16[512,1024]{1,0:T(8,128)(2,1)}) custom-call(bf16[64,64,1024]{2,1,0:T(8,128)(2,1)} %pair_ref.1, s32[64,1024]{1,0:T(8,128)} %bucket_ref.1, f32[1,64]{1,0:T(1,128)} %bitcast.13, bf16[64,256]{1,0:T(8,128)(2,1)} %w_in_ref.5, ...), custom_call_target="tpu_custom_call" | custom-call | flops 8589934592 | bytes 41943040 | tf_op jit(solution)/shard_map/pair_forward/pallas_call | solution.py:183
  33.7 4.8 %all-to-all-done = bf16[8,1,64,1152]{3,2,1,0:T(8,128)(2,1)S(1)} async-done(((bf16[8,1,64,1152]{3,2,1,0:T(8,128)(2,1)}), bf16[8,1,64,1152]{3,2,1,0:T(8,128)(2,1)S(1)}, u32[]{:S(2)}, u32[]{:S(2)}) %all-to-all-start) | async-done | bytes 1179680 | tf_op jit(solution)/shard_map/all_to_all | solution.py:485
  38.5 0.0 copy-done.1
  38.5 0.0 copy-start.2
  38.5 1.2 %copy-done.2 = bf16[512,1024]{1,0:T(8,128)(2,1)S(1)} copy-done((bf16[512,1024]{1,0:T(8,128)(2,1)S(1)}, bf16[512,1024]{1,0:T(8,128)(2,1)}, u32[]{:S(2)}) %copy-start.2) | copy-done | bytes 1048600
  39.8 5.1 %pair_attention.1 = (bf16[512,1024]{1,0:T(8,128)(2,1)S(1)}, bf16[8,64,1152]{2,1,0:T(8,128)(2,1)}) custom-call(bf16[512,1024]{1,0:T(8,128)(2,1)S(1)} %copy-done.2, bf16[8,64,1152]{2,1,0:T(8,128)(2,1)S(1)} %bitcast.7, bf16[8,64,1152]{2,1,0:T(8,128)(2,1)S(1)} %bitcast.8, s32[1,1024]{1,0:T(1,128)S(1)} %bitcast.9), custom_call_target="tpu_custom_call" | custom-call | flops 1342177280 | bytes 4194304 | tf_op jit(solution)/shard_map/pair_attention/pallas_call | solution.py:303
  44.8 0.0 copy-start
  44.8 1.0 %copy-done = bf16[512,1024]{1,0:T(8,128)(2,1)} copy-done((bf16[512,1024]{1,0:T(8,128)(2,1)}, bf16[512,1024]{1,0:T(8,128)(2,1)S(1)}, u32[]{:S(2)}) %copy-start) | copy-done | bytes 1048600
  45.9 3.7 %all-to-all-start.1 = ((bf16[8,1,64,1152]{3,2,1,0:T(8,128)(2,1)}), bf16[8,1,64,1152]{3,2,1,0:T(8,128)(2,1)S(1)}, u32[]{:S(2)}, u32[]{:S(2)}) async-start(bf16[8,1,64,1152]{3,2,1,0:T(8,128)(2,1)} %bitcast.6), calls=%async_computation.1 | async-start | bytes 2359296 | tf_op jit(solution)/shard_map/all_to_all | solution.py:491
  49.5 27.5 %pair_backward.2.rest_0_ = bf16[64,64,1024]{2,1,0:T(8,128)(2,1)} custom-call(bf16[64,8,64,128]{3,2,1,0:T(8,128)(2,1)} %get-tuple-element.20.unit_ref, f32[64,1024]{1,0:T(8,128)} %get-tuple-element.21.inv_ref, bf16[512,1024]{1,0:T(8,128)(2,1)} %copy-done, bf16[64,8,256,128]{3,2,1,0:T(8,128)(2,1)} %get-tuple-element.24.scaled_ref, f32[1,64]{1,0:T(1,128)} %bitcast.14, ...), custom_call_target="tpu_custom_call" | custom-call | flops 7516192768 | bytes 44040192 | tf_op jit(solution)/shard_map/pair_backward/pallas_call | solution.py:394
  77.0 1.2 %all-to-all-done.1.part_ref = bf16[8,1,64,1152]{3,2,1,0:T(8,128)(2,1)S(1)} async-done(((bf16[8,1,64,1152]{3,2,1,0:T(8,128)(2,1)}), bf16[8,1,64,1152]{3,2,1,0:T(8,128)(2,1)S(1)}, u32[]{:S(2)}, u32[]{:S(2)}) %all-to-all-start.1) | async-done | bytes 1179680 | tf_op jit(solution)/shard_map/all_to_all | solution.py:491
  78.3 0.2 sum_sources.1
  78.5 0.1 collective-permute-start
  78.5 1.6 %collective-permute-start.1 = (f32[1,32,512]{2,1,0:T(8,128)S(1)}, f32[1,32,512]{2,1,0:T(8,128)S(1)}, u32[]{:S(2)}, u32[]{:S(2)}) collective-permute-start(f32[1,32,512]{2,1,0:T(8,128)S(1)} %get-tuple-element.32.dq_ref), channel_id=1, source_target_pairs={{0,8},{8,0},{1,9},{9,1},{2,10},{10,2},{3,11},{11,3},{4,12},{12,4},... | collective-permute-start | bytes 196616 | tf_op jit(solution)/shard_map/ppermute | solution.py:78
  80.1 6.7 %pair_backward.3 = bf16[64,64,1024]{2,1,0:T(8,128)(2,1)} custom-call(bf16[64,8,64,128]{3,2,1,0:T(8,128)(2,1)} %get-tuple-element.20.unit_ref, f32[64,1024]{1,0:T(8,128)} %get-tuple-element.21.inv_ref, bf16[512,1024]{1,0:T(8,128)(2,1)} %copy-done, bf16[64,8,256,128]{3,2,1,0:T(8,128)(2,1)} %get-tuple-element.24.scaled_ref, ...), custom_call_target="tpu_custom_call", output_to_operand_aliasing={{}: (7, {})} | custom-call | flops 1073741824 | bytes 6291456 | tf_op jit(solution)/shard_map/pair_backward/pallas_call | solution.py:394
  86.8 0.0 collective-permute-done.1.dq_other
  86.8 0.0 collective-permute-done.dkv_other
  86.8 0.7 finish.1
Async XLA Ops:
  2.7 35.9 %all-to-all-start = ((bf16[8,1,64,1152]{3,2,1,0:T(8,128)(2,1)}), bf16[8,1,64,1152]{3,2,1,0:T(8,128)(2,1)S(1)}, u32[]{:S(2)}, u32[]{:S(2)}) async-start(bf16[8,1,64,1152]{3,2,1,0:T(8,128)(2,1)} %pack_heads.1), calls=%async_computation | async-start | bytes 2359296 | tf_op jit(solution)/shard_map/all_to_all | solution.py:485
  10.0 28.6 %copy-start.1 = (s32[1024]{0:T(1024)S(1)}, s32[1024]{0:T(1024)}, u32[]{:S(2)}) copy-start(s32[1024]{0:T(1024)} %param.21) | copy-start | bytes 12292
  38.5 1.2 %copy-start.2 = (bf16[512,1024]{1,0:T(8,128)(2,1)S(1)}, bf16[512,1024]{1,0:T(8,128)(2,1)}, u32[]{:S(2)}) copy-start(bf16[512,1024]{1,0:T(8,128)(2,1)} %get-tuple-element.22.bias_ref) | copy-start | bytes 3145732
  44.8 1.0 %copy-start = (bf16[512,1024]{1,0:T(8,128)(2,1)}, bf16[512,1024]{1,0:T(8,128)(2,1)S(1)}, u32[]{:S(2)}) copy-start(bf16[512,1024]{1,0:T(8,128)(2,1)S(1)} %get-tuple-element.23.ds_ref) | copy-start | bytes 3145732
  45.9 32.4 %all-to-all-start.1 = ((bf16[8,1,64,1152]{3,2,1,0:T(8,128)(2,1)}), bf16[8,1,64,1152]{3,2,1,0:T(8,128)(2,1)S(1)}, u32[]{:S(2)}, u32[]{:S(2)}) async-start(bf16[8,1,64,1152]{3,2,1,0:T(8,128)(2,1)} %bitcast.6), calls=%async_computation.1 | async-start | bytes 2359296 | tf_op jit(solution)/shard_map/all_to_all | solution.py:491
  78.5 8.4 %collective-permute-start = (f32[1,64,1024]{2,1,0:T(8,128)S(1)}, f32[1,64,1024]{2,1,0:T(8,128)S(1)}, u32[]{:S(2)}, u32[]{:S(2)}) collective-permute-start(f32[1,64,1024]{2,1,0:T(8,128)S(1)} %get-tuple-element.31.dkv_ref), channel_id=1, source_target_pairs={{0,16},{16,0},{1,17},{17,1},{2,18},{18,2},{3,19},{19,3},{4,20},{20... | collective-permute-start | bytes 786440 | tf_op jit(solution)/shard_map/ppermute | solution.py:78
  78.5 8.3 %collective-permute-start.1 = (f32[1,32,512]{2,1,0:T(8,128)S(1)}, f32[1,32,512]{2,1,0:T(8,128)S(1)}, u32[]{:S(2)}, u32[]{:S(2)}) collective-permute-start(f32[1,32,512]{2,1,0:T(8,128)S(1)} %get-tuple-element.32.dq_ref), channel_id=1, source_target_pairs={{0,8},{8,0},{1,9},{9,1},{2,10},{10,2},{3,11},{11,3},{4,12},{12,4},... | collective-permute-start | bytes 196616 | tf_op jit(solution)/shard_map/ppermute | solution.py:78

commit v5 on v4

--- a/solution.py
+++ b/solution.py
@@ -15,6 +15,7 @@
 EXP2_SHIFT = math.log2(2.0 / math.sqrt(math.pi))
 ROWS = 16
 LANES = 128
+READY = 2
 NT = (((1,), (1,)), ((), ()))
 FULL_LIMIT = 60 << 20
 BIG_LIMIT = 32 << 20
@@ -110,6 +111,11 @@
     )(k_heads, v_heads, q_heads, dout_heads, out_heads, log_norm)
 
 
+def slope_of(scaled, cdf2):
+    density2 = jnp.exp2(scaled * scaled * low(EXP2_SCALE) + low(EXP2_SHIFT))
+    return cdf2 + scaled * density2
+
+
 def unit_norm(values):
     centre = values - jnp.mean(values, axis=0, keepdims=True)
     inv_std = lax.rsqrt(jnp.mean(centre * centre, axis=0, keepdims=True) + 1e-05)
@@ -117,8 +123,8 @@
 
 
 def forward_kernel(
-    pair_ref, bucket_ref, gain_ref, w_in_ref, b_in_ref, w_out_ref, table_ref, scaled_ref, unit_ref, inv_ref, bias_ref, w_pre,
-    w_mix, table, gain, *, group, merge
+    pair_ref, bucket_ref, gain_ref, w_in_ref, b_in_ref, w_out_ref, table_ref, saved_ref, unit_ref, inv_ref, bias_ref, w_pre,
+    w_mix, table, gain, *, group, merge, ready
 ):
     rows, chans, keys = pair_ref.shape
     heads, buckets = table_ref.shape
@@ -138,7 +144,7 @@
         table[...] = jnp.dot(table_ref[...], place, preferred_element_type=F32)
         gain[...] = gain_columns(gain_ref[...])
 
-    def some_rows(row):
+    def some_rows(row, with_slope):
         pairs = jnp.concatenate([pair_ref[row + member] for member in range(merge)], axis=1)
         unit_pairs, inv_std = unit_norm(pairs.astype(F32))
         unit_low = unit_pairs.astype(BF16)
@@ -146,8 +152,11 @@
         ones = jnp.where(lax.broadcasted_iota(jnp.int32, (ROWS, width), 0) < 3, 1.0, 0.0).astype(BF16)
         pre_act = jnp.dot(w_pre[...], jnp.concatenate([normed, ones], axis=0), preferred_element_type=F32)
         scaled = pre_act * RSQRT2
-        hidden = (pre_act * (lax.erf(scaled) + 1.0)).astype(BF16)
-        scaled_low = scaled.astype(BF16)
+        cdf2 = lax.erf(scaled) + 1.0
+        hidden = (pre_act * cdf2).astype(BF16)
+        saved = scaled.astype(BF16)
+        if with_slope:
+            saved = slope_of(saved, cdf2.astype(BF16))
         outs = []
         mixed = jnp.dot(w_mix[...], hidden, preferred_element_type=F32)
         for member in range(merge):
@@ -156,7 +165,7 @@
             id_row = bucket_ref[pl.ds(first_row + row + member, 1), :]
             for part in range(keys // LANES):
                 begin = member * keys + part * LANES
-                scaled_ref[row + member, part] = scaled_low[:, begin : begin + LANES]
+                saved_ref[row + member, part] = saved[:, begin : begin + LANES]
                 unit_ref[row + member, part] = unit_low[:, begin : begin + LANES]
                 ids = id_row[:, part * LANES : (part + 1) * LANES]
                 lookup = jnp.take_along_axis(table[...], jnp.broadcast_to(ids, (heads, LANES)), axis=1)
@@ -167,7 +176,7 @@
     def step(index, carry):
         outs = []
         for member in range(0, group, merge):
-            outs += some_rows(index * group + member)
+            outs += some_rows(index * group + member, member < ready)
         size = group * heads
         bias_ref[pl.ds(pl.multiple_of(index * size, size), size), :] = jnp.concatenate(outs, axis=0).astype(BF16)
         return carry
@@ -181,7 +190,7 @@
     block = divisor(rows, 8)
     parts = keys // LANES
     return pl.pallas_call(
-        functools.partial(forward_kernel, group=block, merge=divisor(block, 2)),
+        functools.partial(forward_kernel, group=block, merge=divisor(block, 2), ready=READY),
         grid=(rows // block,),
         in_specs=[
             pl.BlockSpec((block, chans, keys), lambda i: (i, 0, 0)),
@@ -314,7 +323,7 @@
             pl.BlockSpec((heads, depth, keys + LANES), lambda i: (0, 0, 0)),
         ],
         out_shape=[
-            jax.ShapeDtypeStruct((flat, keys), BF16),
+            pltpu.HBM((flat, keys), BF16),
             jax.ShapeDtypeStruct((heads, depth, keys + LANES), BF16),
         ],
         scratch_shapes=[
@@ -331,10 +340,10 @@
             flops=10 * flat * keys * width, bytes_accessed=8 * flat * keys, transcendentals=flat * keys
         ),
         name="pair_attention",
-    )(bias, received, received, key_mask.reshape(1, keys))
-
-
-def backward_kernel(unit_ref, inv_ref, ds_ref, scaled_ref, gain_ref, w_in_ref, w_out_ref, *rest, group, merge):
+    )(pltpu.with_memory_space_constraint(bias, pltpu.HBM), received, received, key_mask.reshape(1, keys))
+
+
+def backward_kernel(unit_ref, inv_ref, ds_ref, saved_ref, gain_ref, w_in_ref, w_out_ref, *rest, group, merge, ready):
     out_ref, w_back, gain = rest[-3:]
     rows, parts, chans, _ = unit_ref.shape
     heads = w_out_ref.shape[0]
@@ -352,11 +361,10 @@
             members = range(begin, begin + merge)
             tiles = [(index * group + member, part) for member in members for part in range(parts)]
             unit_pairs = jnp.concatenate([unit_ref[row, part] for row, part in tiles], axis=1).astype(F32)
-            scaled = jnp.concatenate([scaled_ref[row, part] for row, part in tiles], axis=1)
+            saved = jnp.concatenate([saved_ref[row, part] for row, part in tiles], axis=1)
             inv_std = jnp.concatenate([inv_ref[pl.ds(index * group + member, 1), :] for member in members], axis=1)
             own = [dscores[member * heads : (member + 1) * heads] for member in members]
-            density2 = jnp.exp2(scaled * scaled * low(EXP2_SCALE) + low(EXP2_SHIFT))
-            slope = lax.erf(scaled) + low(1.0) + scaled * density2
+            slope = saved if begin < ready else slope_of(saved, lax.erf(saved) + low(1.0))
             dhidden = jnp.dot(w_back[...], jnp.concatenate(own, axis=1), preferred_element_type=F32)
             dpre = dhidden.astype(BF16) * slope
             dunit = jnp.dot(w_in_ref[...], dpre, preferred_element_type=F32) * widen(gain[...], keys * merge)
@@ -370,13 +378,13 @@
     lax.fori_loop(0, rows // group, step, 0)
 
 
-def backward_call(unit_pairs, inv_std, dscores, scaled, gain, w_in, w_out, begin, count, previous):
+def backward_call(unit_pairs, inv_std, dscores, saved, gain, w_in, w_out, begin, count, previous):
     rows, parts, chans, _ = unit_pairs.shape
     keys = parts * LANES
     heads, hid = w_out.shape
     block = divisor(math.gcd(begin, count), 8)
     first = begin // block
-    operands = [unit_pairs, inv_std, dscores, scaled, gain, w_in, w_out]
+    operands = [unit_pairs, inv_std, dscores, saved, gain, w_in, w_out]
     in_specs = [
         pl.BlockSpec((block, parts, chans, LANES), lambda i: (i + first, 0, 0, 0)),
         pl.BlockSpec((block, keys), lambda i: (i + first, 0)),
@@ -392,7 +400,7 @@
         operands.append(previous)
         in_specs.append(pl.BlockSpec(memory_space=pl.ANY))
     return pl.pallas_call(
-        functools.partial(backward_kernel, group=block, merge=divisor(block, 2)),
+        functools.partial(backward_kernel, group=block, merge=divisor(block, 2), ready=READY),
         grid=(count // block,),
         in_specs=in_specs,
         out_specs=pl.BlockSpec((block, chans, keys), lambda i: (i + first, 0, 0)),
@@ -483,7 +491,7 @@
 
     packed = pack_call(k_heads, v_heads, q_heads, dout_heads, out_heads, log_norm, axis_size, rows)
     received = lax.all_to_all(packed, "heads", split_axis=0, concat_axis=0, tiled=True)
-    scaled, unit_pairs, inv_std, bias_vals = forward_call(
+    saved, unit_pairs, inv_std, bias_vals = forward_call(
         pair_feats, bucket_ids, gain, w_in, b_in.reshape(1, -1), w_out.T, bucket_table.T
     )
     received = received.reshape((axis_size * own_heads,) + received.shape[2:])
@@ -491,15 +499,11 @@
     parts = lax.all_to_all(
         parts.reshape((axis_size, own_heads) + parts.shape[1:]), "heads", split_axis=0, concat_axis=0, tiled=True
     )
-    last = 8
-    weights = (gain, w_in, w_out.T)
-    grad_pairs = backward_call(unit_pairs, inv_std, dscores, scaled, *weights, 0, rows - last, None)
+    grad_pairs = backward_call(unit_pairs, inv_std, dscores, saved, gain, w_in, w_out.T, 0, rows, None)
     parts, grad_pairs = lax.optimization_barrier((parts, grad_pairs))
     dkv_sum, dq_sum = sum_call(parts, head_dim, rows, queries)
-    grad_pairs, dkv_sum, dq_sum = lax.optimization_barrier((grad_pairs, dkv_sum, dq_sum))
     dkv_other = other_sum(dkv_sum, "query")
     dq_other = other_sum(dq_sum, "key")
-    grad_pairs = backward_call(unit_pairs, inv_std, dscores, scaled, *weights, rows - last, last, grad_pairs)
     grad_q, grad_k, grad_v = finish_call(dkv_sum, dkv_other, dq_sum, dq_other)
     return (grad_pairs, grad_q, grad_k, grad_v)
 

time: 87.9 us -> 84.1 us (0.957)
  local copies, waits for them, and re-layouts: 2.25 us -> 0.01 us
  waiting for transfers between devices: 6.05 us -> 4.68 us
    pallas_call x2 -> x1, Pallas kernels: 34.3 us -> 29.4 us  [backward_call(): pl.pallas_call(functools.partial(backward_kernel, group=block, merge=divi...]
    all_to_all x1, waiting for transfers between devices: 4.82 us -> 1.74 us  [per_device(): lax.all_to_all(packed, 'heads', split_axis=0, concat_axis=0, tiled=True)]
    pallas_call x1, Pallas kernels: 23.8 us -> 26.8 us  [forward_call(): pl.pallas_call(functools.partial(forward_kernel, group=block, merge=divis...]
    ppermute x2, waiting for transfers between devices: 0.01 us -> 2.94 us  [other_sum(): return lax.ppermute(values, name, [(0, 1), (1, 0)])]
    unnamed x6 -> x2, local copies, waits for them, and re-layouts: 2.25 us -> 0.01 us
    all_to_all x1, waiting for transfers between devices: 1.22 us -> 0.01 us  [per_device(): lax.all_to_all(parts.reshape((axis_size, own_heads) + parts.shape[1:]), '...]
    pallas_call x1, Pallas kernels: 5.07 us -> 6.11 us  [attention_call(): pl.pallas_call(functools.partial(attention_kernel, head_dim=head_dim, row...]
  transfers between devices with their start and end apart: 4 -> 4, of which waited for: 2 -> 2; matrix products, arithmetic and copies ran while one was open for 0% -> 0% of each run, Pallas kernels for 66% -> 67%
where the time goes in v5:
time: 84.1 us; the launch traced here: 83.8 us
  Pallas kernels  65.2 us (78%)
  starting transfers between devices  13.2 us (16%)
  waiting for transfers between devices  4.68 us (6%)
    pallas_call x1, Pallas kernels, backward_call(): pl.pallas_call(functools.partial(backward_kernel, group=block, merge=divi...  29.4 us
    pallas_call x1, Pallas kernels, forward_call(): pl.pallas_call(functools.partial(forward_kernel, group=block, merge=divis...  26.8 us
    all_to_all x1, starting transfers between devices, per_device(): lax.all_to_all(packed, 'heads', split_axis=0, concat_axis=0, tiled=True)  7.31 us
    pallas_call x1, Pallas kernels, attention_call(): pl.pallas_call(functools.partial(attention_kernel, head_dim=head_dim, row...  6.11 us
    all_to_all x1, starting transfers between devices, per_device(): lax.all_to_all(parts.reshape((axis_size, own_heads) + parts.shape[1:]), '...  4.26 us
    ppermute x2, waiting for transfers between devices, other_sum(): return lax.ppermute(values, name, [(0, 1), (1, 0)])  2.94 us
    pallas_call x1, Pallas kernels, pack_call(): pl.pallas_call(functools.partial(pack_kernel, rows=rows), out_shape=jax.S...  2.02 us
    all_to_all x1, waiting for transfers between devices, per_device(): lax.all_to_all(packed, 'heads', split_axis=0, concat_axis=0, tiled=True)  1.74 us
  transfers between devices with their start and end apart: 4, of which 2 were waited for; matrix products, arithmetic and copies ran while one was open for 0% of the time, Pallas kernels for 67%

profile of v5, /device:TPU:0, one launch (start us, length us, event | category | flops | bytes accessed | tf_op | source)
XLA Modules:
  0.0 83.8 jit_solution(16941051078744547218)
XLA Ops:
  0.6 2.0 %pack_heads.1 = bf16[8,1,64,1152]{3,2,1,0:T(8,128)(2,1)} custom-call(bf16[1,32,1024]{2,1,0:T(8,128)(2,1)} %k_ref.1, bf16[1,32,1024]{2,1,0:T(8,128)(2,1)} %v_ref.1, bf16[1,32,512]{2,1,0:T(8,128)(2,1)} %q_ref.1, bf16[1,32,512]{2,1,0:T(8,128)(2,1)} %dout_ref.1, bf16[1,32,512]{2,1,0:T(8,128)(2,1)} %out_ref.1, f32[1,512]{1,0:T(1,128)} %norm_ref.1), custom_call_target="tpu_custom_call" | custom-call | tf_op jit(solution)/shard_map/pack_heads/pallas_call | solution.py:106
  2.7 7.3 %all-to-all-start = ((bf16[8,1,64,1152]{3,2,1,0:T(8,128)(2,1)}), bf16[8,1,64,1152]{3,2,1,0:T(8,128)(2,1)S(1)}, u32[]{:S(2)}, u32[]{:S(2)}) async-start(bf16[8,1,64,1152]{3,2,1,0:T(8,128)(2,1)} %pack_heads.1), calls=%async_computation | async-start | bytes 2359296 | tf_op jit(solution)/shard_map/all_to_all | solution.py:493
  10.0 0.0 copy-start
  10.0 26.8 %pair_forward.1 = (bf16[64,8,256,128]{3,2,1,0:T(8,128)(2,1)}, bf16[64,8,64,128]{3,2,1,0:T(8,128)(2,1)}, f32[64,1024]{1,0:T(8,128)}, bf16[512,1024]{1,0:T(8,128)(2,1)}) custom-call(bf16[64,64,1024]{2,1,0:T(8,128)(2,1)} %pair_ref.1, s32[64,1024]{1,0:T(8,128)} %bucket_ref.1, f32[1,64]{1,0:T(1,128)} %bitcast.12, bf16[64,256]{1,0:T(8,128)(2,1)} %w_in_ref.3, ...), custom_call_target="tpu_custom_call" | custom-call | flops 8589934592 | bytes 41943040 | tf_op jit(solution)/shard_map/pair_forward/pallas_call | solution.py:192
  36.8 1.7 %all-to-all-done = bf16[8,1,64,1152]{3,2,1,0:T(8,128)(2,1)S(1)} async-done(((bf16[8,1,64,1152]{3,2,1,0:T(8,128)(2,1)}), bf16[8,1,64,1152]{3,2,1,0:T(8,128)(2,1)S(1)}, u32[]{:S(2)}, u32[]{:S(2)}) %all-to-all-start) | async-done | bytes 1179680 | tf_op jit(solution)/shard_map/all_to_all | solution.py:493
  38.5 0.0 copy-done
  38.5 6.1 %pair_attention.1 = (bf16[512,1024]{1,0:T(8,128)(2,1)}, bf16[8,64,1152]{2,1,0:T(8,128)(2,1)}) custom-call(bf16[512,1024]{1,0:T(8,128)(2,1)} %get-tuple-element.17.bias_ref, bf16[8,64,1152]{2,1,0:T(8,128)(2,1)S(1)} %bitcast.7, bf16[8,64,1152]{2,1,0:T(8,128)(2,1)S(1)} %bitcast.8, s32[1,1024]{1,0:T(1,128)S(1)} %bitcast.9), custom_call_target="tpu_custom_call" | custom-call | flops 1342177280 | bytes 4194304 | tf_op jit(solution)/shard_map/pair_attention/pallas_call | solution.py:312
  44.7 4.3 %all-to-all-start.1 = ((bf16[8,1,64,1152]{3,2,1,0:T(8,128)(2,1)}), bf16[8,1,64,1152]{3,2,1,0:T(8,128)(2,1)S(1)}, u32[]{:S(2)}, u32[]{:S(2)}) async-start(bf16[8,1,64,1152]{3,2,1,0:T(8,128)(2,1)} %bitcast.6), calls=%async_computation.1 | async-start | bytes 2359296 | tf_op jit(solution)/shard_map/all_to_all | solution.py:499
  48.9 29.4 %pair_backward.1 = bf16[64,64,1024]{2,1,0:T(8,128)(2,1)} custom-call(bf16[64,8,64,128]{3,2,1,0:T(8,128)(2,1)} %get-tuple-element.19.unit_ref, f32[64,1024]{1,0:T(8,128)} %get-tuple-element.20.inv_ref, bf16[512,1024]{1,0:T(8,128)(2,1)} %get-tuple-element.21.ds_ref, bf16[64,8,256,128]{3,2,1,0:T(8,128)(2,1)} %get-tuple-element.22.saved_ref, f32[1,64]{1,0:T(1,128)} %bitcast.13, ...), custom_call_target="tpu_custom_call" | custom-call | flops 8589934592 | bytes 50331648 | tf_op jit(solution)/shard_map/pair_backward/pallas_call | solution.py:402
  78.3 0.0 all-to-all-done.1.part_ref
  78.3 0.2 sum_sources.1
  78.5 0.1 collective-permute-start
  78.6 1.6 %collective-permute-start.1 = (f32[1,32,512]{2,1,0:T(8,128)S(1)}, f32[1,32,512]{2,1,0:T(8,128)S(1)}, u32[]{:S(2)}, u32[]{:S(2)}) collective-permute-start(f32[1,32,512]{2,1,0:T(8,128)S(1)} %get-tuple-element.26.dq_ref), channel_id=1, source_target_pairs={{0,8},{8,0},{1,9},{9,1},{2,10},{10,2},{3,11},{11,3},{4,12},{12,4},... | collective-permute-start | bytes 196616 | tf_op jit(solution)/shard_map/ppermute | solution.py:79
  80.1 2.9 %collective-permute-done.1.dq_other = f32[1,32,512]{2,1,0:T(8,128)S(1)} collective-permute-done((f32[1,32,512]{2,1,0:T(8,128)S(1)}, f32[1,32,512]{2,1,0:T(8,128)S(1)}, u32[]{:S(2)}, u32[]{:S(2)}) %collective-permute-start.1) | collective-permute-done | bytes 65568 | tf_op jit(solution)/shard_map/ppermute | solution.py:79
  83.1 0.0 collective-permute-done.dkv_other
  83.1 0.7 finish.1
Async XLA Ops:
  2.7 35.9 %all-to-all-start = ((bf16[8,1,64,1152]{3,2,1,0:T(8,128)(2,1)}), bf16[8,1,64,1152]{3,2,1,0:T(8,128)(2,1)S(1)}, u32[]{:S(2)}, u32[]{:S(2)}) async-start(bf16[8,1,64,1152]{3,2,1,0:T(8,128)(2,1)} %pack_heads.1), calls=%async_computation | async-start | bytes 2359296 | tf_op jit(solution)/shard_map/all_to_all | solution.py:493
  10.0 28.6 %copy-start = (s32[1024]{0:T(1024)S(1)}, s32[1024]{0:T(1024)}, u32[]{:S(2)}) copy-start(s32[1024]{0:T(1024)} %param.21) | copy-start | bytes 12292
  44.7 33.6 %all-to-all-start.1 = ((bf16[8,1,64,1152]{3,2,1,0:T(8,128)(2,1)}), bf16[8,1,64,1152]{3,2,1,0:T(8,128)(2,1)S(1)}, u32[]{:S(2)}, u32[]{:S(2)}) async-start(bf16[8,1,64,1152]{3,2,1,0:T(8,128)(2,1)} %bitcast.6), calls=%async_computation.1 | async-start | bytes 2359296 | tf_op jit(solution)/shard_map/all_to_all | solution.py:499
  78.5 4.6 %collective-permute-start = (f32[1,64,1024]{2,1,0:T(8,128)S(1)}, f32[1,64,1024]{2,1,0:T(8,128)S(1)}, u32[]{:S(2)}, u32[]{:S(2)}) collective-permute-start(f32[1,64,1024]{2,1,0:T(8,128)S(1)} %get-tuple-element.25.dkv_ref), channel_id=1, source_target_pairs={{0,16},{16,0},{1,17},{17,1},{2,18},{18,2},{3,19},{19,3},{4,20},{20... | collective-permute-start | bytes 786440 | tf_op jit(solution)/shard_map/ppermute | solution.py:79
  78.6 4.5 %collective-permute-start.1 = (f32[1,32,512]{2,1,0:T(8,128)S(1)}, f32[1,32,512]{2,1,0:T(8,128)S(1)}, u32[]{:S(2)}, u32[]{:S(2)}) collective-permute-start(f32[1,32,512]{2,1,0:T(8,128)S(1)} %get-tuple-element.26.dq_ref), channel_id=1, source_target_pairs={{0,8},{8,0},{1,9},{9,1},{2,10},{10,2},{3,11},{11,3},{4,12},{12,4},... | collective-permute-start | bytes 196616 | tf_op jit(solution)/shard_map/ppermute | solution.py:79

commit v6 on v5

--- a/solution.py
+++ b/solution.py
@@ -308,7 +308,7 @@
     flat, keys = bias.shape
     heads, depth, _ = received.shape
     width = heads * head_dim
-    tile = divisor(keys, 256)
+    tile = divisor(keys, 1024)
     return pl.pallas_call(
         functools.partial(attention_kernel, head_dim=head_dim, rows=rows),
         grid=(keys // tile,),
@@ -502,8 +502,8 @@
     grad_pairs = backward_call(unit_pairs, inv_std, dscores, saved, gain, w_in, w_out.T, 0, rows, None)
     parts, grad_pairs = lax.optimization_barrier((parts, grad_pairs))
     dkv_sum, dq_sum = sum_call(parts, head_dim, rows, queries)
+    dq_other = other_sum(dq_sum, "key")
     dkv_other = other_sum(dkv_sum, "query")
-    dq_other = other_sum(dq_sum, "key")
     grad_q, grad_k, grad_v = finish_call(dkv_sum, dkv_other, dq_sum, dq_other)
     return (grad_pairs, grad_q, grad_k, grad_v)
 

time: 84.1 us -> 82.7 us (0.983)
  Pallas kernels: 65.2 us -> 63.8 us
    pallas_call x1, Pallas kernels: 6.11 us -> 4.69 us  [attention_call(): pl.pallas_call(functools.partial(attention_kernel, head_dim=head_dim, row...]
  transfers between devices with their start and end apart: 4 -> 4, of which waited for: 2 -> 2; matrix products, arithmetic and copies ran while one was open for 0% -> 0% of each run, Pallas kernels for 67% -> 68%
where the time goes in v6:
time: 82.7 us; the launch traced here: 82.3 us
  Pallas kernels  63.8 us (77%)
  starting transfers between devices  13.2 us (16%)
  waiting for transfers between devices  4.68 us (6%)
    pallas_call x1, Pallas kernels, backward_call(): pl.pallas_call(functools.partial(backward_kernel, group=block, merge=divi...  29.4 us
    pallas_call x1, Pallas kernels, forward_call(): pl.pallas_call(functools.partial(forward_kernel, group=block, merge=divis...  26.8 us
    all_to_all x1, starting transfers between devices, per_device(): lax.all_to_all(packed, 'heads', split_axis=0, concat_axis=0, tiled=True)  7.31 us
    pallas_call x1, Pallas kernels, attention_call(): pl.pallas_call(functools.partial(attention_kernel, head_dim=head_dim, row...  4.69 us
    all_to_all x1, starting transfers between devices, per_device(): lax.all_to_all(parts.reshape((axis_size, own_heads) + parts.shape[1:]), '...  4.24 us
    ppermute x2, waiting for transfers between devices, other_sum(): return lax.ppermute(values, name, [(0, 1), (1, 0)])  2.94 us
    pallas_call x1, Pallas kernels, pack_call(): pl.pallas_call(functools.partial(pack_kernel, rows=rows), out_shape=jax.S...  2.02 us
    all_to_all x1, waiting for transfers between devices, per_device(): lax.all_to_all(packed, 'heads', split_axis=0, concat_axis=0, tiled=True)  1.74 us
  transfers between devices with their start and end apart: 4, of which 2 were waited for; matrix products, arithmetic and copies ran while one was open for 0% of the time, Pallas kernels for 68%

profile of v6, /device:TPU:0, one launch (start us, length us, event | category | flops | bytes accessed | tf_op | source)
XLA Modules:
  0.0 82.3 jit_solution(7547654726629765747)
XLA Ops:
  0.6 2.0 %pack_heads.1 = bf16[8,1,64,1152]{3,2,1,0:T(8,128)(2,1)} custom-call(bf16[1,32,1024]{2,1,0:T(8,128)(2,1)} %k_ref.1, bf16[1,32,1024]{2,1,0:T(8,128)(2,1)} %v_ref.1, bf16[1,32,512]{2,1,0:T(8,128)(2,1)} %q_ref.1, bf16[1,32,512]{2,1,0:T(8,128)(2,1)} %dout_ref.1, bf16[1,32,512]{2,1,0:T(8,128)(2,1)} %out_ref.1, f32[1,512]{1,0:T(1,128)} %norm_ref.1), custom_call_target="tpu_custom_call" | custom-call | tf_op jit(solution)/shard_map/pack_heads/pallas_call | solution.py:106
  2.7 7.3 %all-to-all-start = ((bf16[8,1,64,1152]{3,2,1,0:T(8,128)(2,1)}), bf16[8,1,64,1152]{3,2,1,0:T(8,128)(2,1)S(1)}, u32[]{:S(2)}, u32[]{:S(2)}) async-start(bf16[8,1,64,1152]{3,2,1,0:T(8,128)(2,1)} %pack_heads.1), calls=%async_computation | async-start | bytes 2359296 | tf_op jit(solution)/shard_map/all_to_all | solution.py:493
  10.0 0.0 copy-start
  10.0 26.8 %pair_forward.1 = (bf16[64,8,256,128]{3,2,1,0:T(8,128)(2,1)}, bf16[64,8,64,128]{3,2,1,0:T(8,128)(2,1)}, f32[64,1024]{1,0:T(8,128)}, bf16[512,1024]{1,0:T(8,128)(2,1)}) custom-call(bf16[64,64,1024]{2,1,0:T(8,128)(2,1)} %pair_ref.1, s32[64,1024]{1,0:T(8,128)} %bucket_ref.1, f32[1,64]{1,0:T(1,128)} %bitcast.12, bf16[64,256]{1,0:T(8,128)(2,1)} %w_in_ref.3, ...), custom_call_target="tpu_custom_call" | custom-call | flops 8589934592 | bytes 41943040 | tf_op jit(solution)/shard_map/pair_forward/pallas_call | solution.py:192
  36.8 1.7 %all-to-all-done = bf16[8,1,64,1152]{3,2,1,0:T(8,128)(2,1)S(1)} async-done(((bf16[8,1,64,1152]{3,2,1,0:T(8,128)(2,1)}), bf16[8,1,64,1152]{3,2,1,0:T(8,128)(2,1)S(1)}, u32[]{:S(2)}, u32[]{:S(2)}) %all-to-all-start) | async-done | bytes 1179680 | tf_op jit(solution)/shard_map/all_to_all | solution.py:493
  38.5 0.0 copy-done
  38.5 4.7 %pair_attention.1 = (bf16[512,1024]{1,0:T(8,128)(2,1)}, bf16[8,64,1152]{2,1,0:T(8,128)(2,1)}) custom-call(bf16[512,1024]{1,0:T(8,128)(2,1)} %get-tuple-element.17.bias_ref, bf16[8,64,1152]{2,1,0:T(8,128)(2,1)S(1)} %bitcast.7, bf16[8,64,1152]{2,1,0:T(8,128)(2,1)S(1)} %bitcast.8, s32[1,1024]{1,0:T(1,128)S(1)} %bitcast.9), custom_call_target="tpu_custom_call" | custom-call | flops 1342177280 | bytes 4194304 | tf_op jit(solution)/shard_map/pair_attention/pallas_call | solution.py:312
  43.2 4.2 %all-to-all-start.1 = ((bf16[8,1,64,1152]{3,2,1,0:T(8,128)(2,1)}), bf16[8,1,64,1152]{3,2,1,0:T(8,128)(2,1)S(1)}, u32[]{:S(2)}, u32[]{:S(2)}) async-start(bf16[8,1,64,1152]{3,2,1,0:T(8,128)(2,1)} %bitcast.6), calls=%async_computation.1 | async-start | bytes 2359296 | tf_op jit(solution)/shard_map/all_to_all | solution.py:499
  47.5 29.4 %pair_backward.1 = bf16[64,64,1024]{2,1,0:T(8,128)(2,1)} custom-call(bf16[64,8,64,128]{3,2,1,0:T(8,128)(2,1)} %get-tuple-element.19.unit_ref, f32[64,1024]{1,0:T(8,128)} %get-tuple-element.20.inv_ref, bf16[512,1024]{1,0:T(8,128)(2,1)} %get-tuple-element.21.ds_ref, bf16[64,8,256,128]{3,2,1,0:T(8,128)(2,1)} %get-tuple-element.22.saved_ref, f32[1,64]{1,0:T(1,128)} %bitcast.13, ...), custom_call_target="tpu_custom_call" | custom-call | flops 8589934592 | bytes 50331648 | tf_op jit(solution)/shard_map/pair_backward/pallas_call | solution.py:402
  76.9 0.0 all-to-all-done.1.part_ref
  76.9 0.2 sum_sources.1
  77.0 0.1 collective-permute-start
  77.1 1.6 %collective-permute-start.1 = (f32[1,32,512]{2,1,0:T(8,128)S(1)}, f32[1,32,512]{2,1,0:T(8,128)S(1)}, u32[]{:S(2)}, u32[]{:S(2)}) collective-permute-start(f32[1,32,512]{2,1,0:T(8,128)S(1)} %get-tuple-element.26.dq_ref), channel_id=1, source_target_pairs={{0,8},{8,0},{1,9},{9,1},{2,10},{10,2},{3,11},{11,3},{4,12},{12,4},... | collective-permute-start | bytes 196616 | tf_op jit(solution)/shard_map/ppermute | solution.py:79
  78.7 2.9 %collective-permute-done.1.dq_other = f32[1,32,512]{2,1,0:T(8,128)S(1)} collective-permute-done((f32[1,32,512]{2,1,0:T(8,128)S(1)}, f32[1,32,512]{2,1,0:T(8,128)S(1)}, u32[]{:S(2)}, u32[]{:S(2)}) %collective-permute-start.1) | collective-permute-done | bytes 65568 | tf_op jit(solution)/shard_map/ppermute | solution.py:79
  81.6 0.0 collective-permute-done.dkv_other
  81.6 0.7 finish.1
Async XLA Ops:
  2.7 35.9 %all-to-all-start = ((bf16[8,1,64,1152]{3,2,1,0:T(8,128)(2,1)}), bf16[8,1,64,1152]{3,2,1,0:T(8,128)(2,1)S(1)}, u32[]{:S(2)}, u32[]{:S(2)}) async-start(bf16[8,1,64,1152]{3,2,1,0:T(8,128)(2,1)} %pack_heads.1), calls=%async_computation | async-start | bytes 2359296 | tf_op jit(solution)/shard_map/all_to_all | solution.py:493
  10.0 28.6 %copy-start = (s32[1024]{0:T(1024)S(1)}, s32[1024]{0:T(1024)}, u32[]{:S(2)}) copy-start(s32[1024]{0:T(1024)} %param.21) | copy-start | bytes 12292
  43.2 33.6 %all-to-all-start.1 = ((bf16[8,1,64,1152]{3,2,1,0:T(8,128)(2,1)}), bf16[8,1,64,1152]{3,2,1,0:T(8,128)(2,1)S(1)}, u32[]{:S(2)}, u32[]{:S(2)}) async-start(bf16[8,1,64,1152]{3,2,1,0:T(8,128)(2,1)} %bitcast.6), calls=%async_computation.1 | async-start | bytes 2359296 | tf_op jit(solution)/shard_map/all_to_all | solution.py:499
  77.0 4.6 %collective-permute-start = (f32[1,64,1024]{2,1,0:T(8,128)S(1)}, f32[1,64,1024]{2,1,0:T(8,128)S(1)}, u32[]{:S(2)}, u32[]{:S(2)}) collective-permute-start(f32[1,64,1024]{2,1,0:T(8,128)S(1)} %get-tuple-element.25.dkv_ref), channel_id=1, source_target_pairs={{0,16},{16,0},{1,17},{17,1},{2,18},{18,2},{3,19},{19,3},{4,20},{20... | collective-permute-start | bytes 786440 | tf_op jit(solution)/shard_map/ppermute | solution.py:79
  77.1 4.5 %collective-permute-start.1 = (f32[1,32,512]{2,1,0:T(8,128)S(1)}, f32[1,32,512]{2,1,0:T(8,128)S(1)}, u32[]{:S(2)}, u32[]{:S(2)}) collective-permute-start(f32[1,32,512]{2,1,0:T(8,128)S(1)} %get-tuple-element.26.dq_ref), channel_id=1, source_target_pairs={{0,8},{8,0},{1,9},{9,1},{2,10},{10,2},{3,11},{11,3},{4,12},{12,4},... | collective-permute-start | bytes 196616 | tf_op jit(solution)/shard_map/ppermute | solution.py:79
